TPU v7x, 128 devices: a whole 4x4x4 slice. The times are simulated.
128 devices in a mesh: lat: 8 (over z, core), lon: 16 (over x, y).
Axes of the slice: x: 4, y: 4, z: 4, core: 2. Of those that a mesh axis runs over, the one named last changes fastest.
Arguments:
- sensitivity: bfloat16 [8, 16, 60, 256, 128], P('lat', 'lon'), may hold values from 0 to 0.07470703
- block_ids: int32 [8, 16, 60], P('lat', 'lon'), may hold values from 0 to 131071, as said below
- block_offsets: int32 [8, 16, 4], P('lat', 'lon'), may hold values from 0 to 60, as said below
- ray_counts: int32 [8, 16], P('lat', 'lon'), may hold values from 1 to 768, as said below
- ray_vector: float32 [4, 8, 16, 768], P(None, 'lat', 'lon'), may hold values from -6 to 6
- damping_vector: float32 [4, 256, 512, 128], P(None, 'lat', 'lon'), may hold values from -6 to 6
- model_vector: float32 [4, 256, 512, 128], P(None, 'lat', 'lon'), may hold values from -6 to 6
- solution: float32 [4, 256, 512, 128], P(None, 'lat', 'lon'), may hold values from -6 to 6
- search: float32 [4, 256, 512, 128], P(None, 'lat', 'lon'), may hold values from -6 to 6
- recurrence: float32 [3, 4], replicated, may hold values from 0.5 to 1.5
Outputs:
- ray_out: float32 [4, 8, 16, 768], P(None, 'lat', 'lon')
- damp_out: float32 [4, 256, 512, 128], P(None, 'lat', 'lon')
- model_out: float32 [4, 256, 512, 128], P(None, 'lat', 'lon')
- solution_out: float32 [4, 256, 512, 128], P(None, 'lat', 'lon')
- search_out: float32 [4, 256, 512, 128], P(None, 'lat', 'lon')
- recurrence_out: float32 [3, 4], replicated
Inputs may be any that keep to these rules, and one draw needn't show every extreme that they name: `block_ids`: of the 60 entries of one device at most 2 name blocks of one owner device; some owner is named exactly 2 times by every device. Entries of tiles that belong to no ray block name blocks too. The entries of all devices that name one owner's blocks lie in one patch of 4 x 4 neighbouring columns of that owner. `block_offsets`: each device's offsets start at 0 and never fall; a ray block holding some live ray has 10 to 20 tiles, the others none; some device uses all 60 tiles. A device's live rays are its first ray_counts rays; some device has all 768 live.
All inputs are finite; a program needn't handle non-finite values.
Results may differ from a plain program's by a relative error of at most 0.0003.
Values may be sent and summed in bfloat16 or wider, within the bound.
A program may use at most 64 MiB of HBM per device.

v0:
```python
import jax
import jax.numpy as jnp
from jax import lax
from jax.sharding import PartitionSpec as P

DAMP_WEIGHT = 0.15
EPSILON = 1e-05
HIGHEST_PRECISION = lax.Precision.HIGHEST


def with_halo(cells, sides, width):
    for axis, dim in sides:
        count = lax.axis_size(axis)
        ends = count - 1
        head = lax.slice_in_dim(cells, 0, width, axis=dim)
        tail = lax.slice_in_dim(cells, cells.shape[dim] - width, cells.shape[dim], axis=dim)
        cells = jnp.concatenate(
            [
                lax.ppermute(tail, axis, [(i, (i + 1) % count) for i in range(ends)]),
                cells,
                lax.ppermute(head, axis, [((i + 1) % count, i) for i in range(ends)]),
            ],
            axis=dim,
        )
    return cells


def laplace(field):
    padded = with_halo(field, (("lat", 1), ("lon", 2)), 1)
    depth_pad = jnp.pad(field, ((0, 0), (0, 0), (0, 0), (1, 1)))
    beside_all = (
        padded[:, 2:, 1:-1] + padded[:, :-2, 1:-1] + padded[:, 1:-1, 2:] + padded[:, 1:-1, :-2]
    )
    beside_all = beside_all + depth_pad[..., 2:] + depth_pad[..., :-2]
    return 6.0 * field - beside_all


def membership(limits, tiles):
    position = jnp.arange(tiles, dtype=jnp.int32)[:, None]
    inside = (position >= limits[None, :-1]) & (position < limits[None, 1:])
    return inside.astype(jnp.float32)


def per_device(
    sensitivity,
    block_ids,
    block_offsets,
    ray_counts,
    ray_vector,
    damping_vector,
    model_vector,
    solution,
    search,
    recurrence,
):
    lat_size = lax.axis_size("lat")
    lon_size = lax.axis_size("lon")
    devices = lat_size * lon_size
    kernel = sensitivity[0, 0]
    tiles, ray_width, depth = kernel.shape
    block_list = block_ids[0, 0]
    bounds = block_offsets[0, 0]
    count_here = ray_counts[0, 0]
    blocks_dev = bounds.shape[0] - 1
    systems, clat_dev, clon_dev = (
        model_vector.shape[0],
        model_vector.shape[1],
        model_vector.shape[2],
    )
    columns_dev = clat_dev * clon_dev
    capacity = 2 * ((tiles + devices - 1) // devices)
    cells_all = devices * columns_dev * depth
    rows_all = devices * blocks_dev * ray_width + cells_all
    alpha_old = recurrence[0]
    rho_bar = recurrence[1]
    phi_bar = recurrence[2]
    owner_dev = block_list // columns_dev
    column = block_list - owner_dev * columns_dev
    owner_hits = (owner_dev[:, None] == jnp.arange(devices, dtype=jnp.int32)[None, :]).astype(
        jnp.int32
    )
    slot_rank = jnp.sum(owner_hits * (jnp.cumsum(owner_hits, axis=0) - 1), axis=1)
    slot_index = owner_dev * capacity + slot_rank
    request = jnp.zeros((devices * capacity,), jnp.int32).at[slot_index].set(column + 1)
    wanted = lax.all_to_all(request, ("lat", "lon"), split_axis=0, concat_axis=0, tiled=True)
    table = (
        model_vector.transpose(1, 2, 0, 3).reshape(columns_dev, systems, depth).astype(jnp.bfloat16)
    )
    served = jnp.where(
        (wanted > 0)[:, None, None],
        jnp.take(table, jnp.maximum(wanted - 1, 0), axis=0),
        jnp.zeros((), jnp.bfloat16),
    )
    fetched = lax.all_to_all(served, ("lat", "lon"), split_axis=0, concat_axis=0, tiled=True)
    tile_model = jnp.take(fetched, slot_index, axis=0)
    member = membership(bounds, tiles)
    products = jnp.einsum("tid,trd->tri", kernel, tile_model, preferred_element_type=jnp.float32)
    traced = jnp.einsum("tb,tri->rbi", member, products, precision=HIGHEST_PRECISION)
    ray_old = ray_vector.reshape(systems, blocks_dev, ray_width)
    ray_index = jnp.arange(blocks_dev * ray_width, dtype=jnp.int32).reshape(blocks_dev, ray_width)
    live_rows = ray_index < count_here
    ray_bar = jnp.where(live_rows[None], traced - alpha_old[:, None, None] * ray_old, 0.0)
    damp_bar = DAMP_WEIGHT * laplace(model_vector) - alpha_old[:, None, None, None] * damping_vector
    residual_sq = jnp.sum(ray_bar * ray_bar, axis=(1, 2)) + jnp.sum(
        damp_bar * damp_bar, axis=(1, 2, 3)
    )
    ray_low = ray_bar.astype(jnp.bfloat16)
    spread = jnp.einsum(
        "tb,rbi->tri", member.astype(jnp.bfloat16), ray_low, preferred_element_type=jnp.float32
    ).astype(jnp.bfloat16)
    sent_terms = jnp.einsum("tid,tri->trd", kernel, spread, preferred_element_type=jnp.float32)
    outgoing = (
        jnp.zeros((devices * capacity, systems, depth), jnp.float32).at[slot_index].set(sent_terms)
    )
    incoming = lax.all_to_all(outgoing, ("lat", "lon"), split_axis=0, concat_axis=0, tiled=True)
    collected = jnp.zeros((columns_dev + 1, systems, depth), jnp.float32).at[wanted].add(incoming)
    remote_part = collected[1:].reshape(clat_dev, clon_dev, systems, depth).transpose(2, 0, 1, 3)
    adjoint_image = remote_part + DAMP_WEIGHT * laplace(damp_bar)
    residual_sq = lax.psum(residual_sq, ("lat", "lon"))
    beta_new = jnp.sqrt(residual_sq / rows_all + EPSILON)
    beta_wide = beta_new[:, None, None, None]
    update = adjoint_image / beta_wide - beta_wide * model_vector
    update_sq = lax.psum(jnp.sum(update * update, axis=(1, 2, 3)), ("lat", "lon"))
    alpha_new = jnp.sqrt(update_sq / cells_all + EPSILON)
    model_out = update / alpha_new[:, None, None, None]
    rho_new = jnp.sqrt(rho_bar * rho_bar + beta_new * beta_new)
    cosine = rho_bar / rho_new
    sine_new = beta_new / rho_new
    solution_out = solution + (cosine * phi_bar / rho_new)[:, None, None, None] * search
    search_out = model_out - (sine_new * alpha_new / rho_new)[:, None, None, None] * search
    ray_out = (ray_bar / beta_new[:, None, None]).reshape(systems, 1, 1, blocks_dev * ray_width)
    damp_out = damp_bar / beta_wide
    recurrence_out = jnp.stack([alpha_new, -cosine * alpha_new, sine_new * phi_bar])
    return (ray_out, damp_out, model_out, solution_out, search_out, recurrence_out)


def solution(mesh):
    return jax.shard_map(
        per_device,
        mesh=mesh,
        in_specs=(
            P("lat", "lon", None, None, None),
            P("lat", "lon", None),
            P("lat", "lon", None),
            P("lat", "lon"),
            P(None, "lat", "lon", None),
            P(None, "lat", "lon", None),
            P(None, "lat", "lon", None),
            P(None, "lat", "lon", None),
            P(None, "lat", "lon", None),
            P(),
        ),
        out_specs=(
            P(None, "lat", "lon", None),
            P(None, "lat", "lon", None),
            P(None, "lat", "lon", None),
            P(None, "lat", "lon", None),
            P(None, "lat", "lon", None),
            P(),
        ),
        check_vma=False,
    )
```

profile of v0, /device:TPU:1, one launch (start us, length us, event | category | flops | bytes accessed | tf_op | source)
XLA Modules:
  0.0 287.2 jit_solution(6578897297421727996)
XLA Ops:
  0.7 0.8 fusion.41
  1.8 0.7 fusion.36
  2.5 0.8 scatter_custom_fusion
  3.3 0.8 all_to_all.14
  4.0 11.5 %all-to-all-start = ((s32[128,2,1]{1,2,0:T(1,128)}), s32[128,2,1]{1,2,0:T(1,128)S(1)}, u32[]{:S(2)}, u32[]{:S(2)}) async-start(s32[128,2,1]{1,2,0:T(1,128)} %bitcast.5), calls=%async_computation | async-start | bytes 131072 | tf_op jit(solution)/shard_map/all_to_all | solution.py:85
  15.5 1.5 fusion.54
  17.1 3.0 %collective-permute-start = (f32[4,1,32,128]{3,1,2,0:T(1,128)}, f32[4,1,32,128]{3,1,2,0:T(1,128)S(1)}, u32[]{:S(2)}, u32[]{:S(2)}) collective-permute-start(f32[4,1,32,128]{3,1,2,0:T(1,128)} %bitcast.16), channel_id=1, source_target_pairs={{16,0},{32,16},{48,32},{64,48},{80,64},{96,80},{112,96},{17,1},{33... | collective-permute-start | bytes 196616 | tf_op jit(solution)/shard_map/ppermute | solution.py:21
  20.0 2.6 collective-permute-start.1
  22.6 1.8 convert_bitcast_fusion
  24.5 0.6 pad_clamp_fusion
  25.6 1.2 slice_bitcast_fusion
  26.8 0.6 slice_bitcast_fusion.2
  28.7 2.5 copy.27
  31.2 0.8 copy.23
  32.6 0.8 reduce.7
  34.6 0.7 le.29
  35.2 0.6 gt.11
  35.9 1.0 gather_fusion
  36.9 0.9 pad_maximum_fusion.21
  37.8 3.2 %collective-permute-start.3 = (f32[4,34,1,128]{3,1,2,0:T(8,128)S(1)}, f32[4,34,1,128]{3,1,2,0:T(8,128)S(1)}, u32[]{:S(2)}, u32[]{:S(2)}) collective-permute-start(f32[4,34,1,128]{3,1,2,0:T(8,128)S(1)} %get-tuple-element.42), channel_id=1, source_target_pairs={{0,1},{1,2},{2,3},{3,4},{4,5},{5,6},{6,7},{7,8},{8,9},{9,10},{10,1... | collective-permute-start | bytes 208904 | tf_op jit(solution)/shard_map/ppermute | solution.py:19
  41.1 1.3 collective-permute-start.2
  42.4 2.1 select_select_fusion
  44.5 10.2 %all-to-all-start.1 = ((bf16[256,4,128]{2,1,0:T(4,128)(2,1)}), bf16[256,4,128]{2,1,0:T(4,128)(2,1)S(1)}, u32[]{:S(2)}, u32[]{:S(2)}) async-start(bf16[256,4,128]{2,1,0:T(4,128)(2,1)} %select_select_fusion), calls=%async_computation.1 | async-start | bytes 524288 | tf_op jit(solution)/shard_map/all_to_all | solution.py:94
  54.8 9.8 %multiply_reduce_fusion.1 = (f32[4]{0:T(128)S(1)}, f32[4,32,32,128]{3,1,2,0:T(8,128)S(1)}) fusion(f32[4,32,32,128]{3,2,1,0:T(8,128)} %param.15, f32[4]{0:T(128)S(1)} %copy-done.10, f32[4,32,32,128]{3,1,2,0:T(8,128)} %copy.27, f32[4,1,32,128]{3,1,2,0:T(1,128)S(1)} %collective-permute-done, f32[4,1,32,128]{3,1,2,0:T(1,128)S(1)} %collective-permute-done.1, ...), kind=kLoop, calls=%fused_computation.52 | loop fusion | flops 10485756 | bytes 6561824 | tf_op jit(solution)/shard_map/reduce_sum | solution.py:104
  64.6 1.3 copy-done.1
  66.0 3.0 %collective-permute-start.4 = (f32[4,1,32,128]{3,1,2,0:T(1,128)S(1)}, f32[4,1,32,128]{3,1,2,0:T(1,128)S(1)}, u32[]{:S(2)}, u32[]{:S(2)}) collective-permute-start(f32[4,1,32,128]{3,1,2,0:T(1,128)S(1)} %get-tuple-element.45), channel_id=1, source_target_pairs={{16,0},{32,16},{48,32},{64,48},{80,64},{96,80},{112,96},{17,1},{33... | collective-permute-start | bytes 196616 | tf_op jit(solution)/shard_map/ppermute | solution.py:21
  68.9 2.6 collective-permute-start.5
  71.6 0.8 gather_fusion.1
  72.4 3.4 %fusion.2 = f32[60,4,256]{2,1,0:T(4,128)S(1)} fusion(bf16[1,1,60,256,128]{4,3,2,1,0:T(8,128)(2,1)} %param.10, bf16[60,4,128]{2,1,0:T(4,128)(2,1)S(1)} %gather_fusion.1, pred[60]{0:T(512)(128)(4,1)S(1)} %copy-done.17), kind=kOutput, calls=%fused_computation.11 | convolution fusion | flops 15759360 | bytes 4239420 | tf_op jit(solution)/shard_map/tid,trd->tri/dot_general | solution.py:97
  76.5 0.6 fusion
  77.1 0.9 broadcast_in_dim.74
  78.0 6.9 %scatter_fusion = f32[256,4,128]{2,1,0:T(4,128)} fusion(f32[256,4,128]{2,1,0:T(4,128)} %broadcast_in_dim.74, s32[60]{0:T(128)S(1)} %copy-done.12, f32[60,4,128]{2,1,0:T(4,128)S(1)} %fusion), kind=kCustom, calls=%fused_computation.3 | custom fusion | bytes 368880 | tf_op jit(solution)/shard_map/scatter | solution.py:113
  84.9 9.5 %all-to-all-start.2 = ((f32[256,4,128]{2,1,0:T(4,128)}), f32[256,4,128]{2,1,0:T(4,128)S(1)}, u32[]{:S(2)}, u32[]{:S(2)}) async-start(f32[256,4,128]{2,1,0:T(4,128)} %scatter_fusion), calls=%async_computation.2 | async-start | bytes 1048576 | tf_op jit(solution)/shard_map/all_to_all | solution.py:115
  94.4 0.9 pad_maximum_fusion.18
  95.3 3.3 %collective-permute-start.7 = (f32[4,34,1,128]{3,1,2,0:T(8,128)S(1)}, f32[4,34,1,128]{3,1,2,0:T(8,128)S(1)}, u32[]{:S(2)}, u32[]{:S(2)}) collective-permute-start(f32[4,34,1,128]{3,1,2,0:T(8,128)S(1)} %get-tuple-element.40), channel_id=1, source_target_pairs={{0,1},{1,2},{2,3},{3,4},{4,5},{5,6},{6,7},{7,8},{8,9},{9,10},{10,1... | collective-permute-start | bytes 208904 | tf_op jit(solution)/shard_map/ppermute | solution.py:19
  98.6 1.3 collective-permute-start.6
  99.9 68.6 %psum.14 = f32[4]{0:T(128)S(1)} all-reduce(f32[4]{0:T(128)S(1)} %add.158), channel_id=1, replica_groups=mesh['lat'=8,'lon'=16] {'lat','lon'}, use_global_device_ids=true, to_apply=%region_5.6 | all-reduce | flops 4 | bytes 32 | tf_op jit(solution)/shard_map/psum | solution.py:119
  168.6 0.6 reshape.267
  169.3 1.5 broadcast_in_dim.73
  170.7 31.4 %scatter_fusion.1 = f32[1025,4,128]{2,1,0:T(4,128)} fusion(f32[1025,4,128]{2,1,0:T(4,128)} %broadcast_in_dim.73, s32[256]{0:T(256)S(1)} %bitcast.95, f32[256,4,128]{2,1,0:T(4,128)S(1)} %all-to-all-done.2), kind=kCustom, calls=%fused_computation.4 | custom fusion | flops 131072 | bytes 1573888 | tf_op jit(solution)/shard_map/scatter-add | solution.py:116
  202.1 1.9 slice.118
  204.3 5.9 %multiply_reduce_fusion = (f32[4]{0:T(128)S(1)}, f32[4,32,32,128]{3,1,2,0:T(8,128)}, f32[4,32,32,128]{3,1,2,0:T(8,128)S(1)}) fusion(f32[4,32,32,128]{3,2,1,0:T(8,128)S(1)} %copy-done, f32[4]{0:T(128)S(1)} %add_sqrt_fusion.1, f32[4,32,32,128]{3,1,2,0:T(8,128)S(1)} %copy-done.2, f32[4,1,32,128]{3,1,2,0:T(1,128)S(1)} %collective-permute-done.4, ...), kind=kLoop, calls=%fused_computation.51 | loop fusion | flops 12058620 | bytes 10756128 | tf_op jit(solution)/shard_map/reduce_sum | solution.py:123
  210.2 2.5 copy.40
  212.7 63.9 %psum.15 = f32[4]{0:T(128)S(1)} all-reduce(f32[4]{0:T(128)S(1)} %get-tuple-element.33), channel_id=1, replica_groups=mesh['lat'=8,'lon'=16] {'lat','lon'}, use_global_device_ids=true, to_apply=%region_9.10 | all-reduce | flops 4 | bytes 32 | tf_op jit(solution)/shard_map/psum | solution.py:123
  276.7 2.9 %fusion.22 = (f32[4,32,32,128]{3,1,2,0:T(8,128)S(1)}, f32[4,32,32,128]{3,1,2,0:T(8,128)S(1)}) fusion(f32[4,32,32,128]{3,2,1,0:T(8,128)S(1)} %copy-done.4, f32[4]{0:T(128)S(1)} %get-tuple-element.52, f32[4,32,32,128]{3,1,2,0:T(8,128)} %get-tuple-element.34, f32[4]{0:T(128)S(1)} %get-tuple-element.53), kind=kLoop, calls=%fused_computation.48 | loop fusion | flops 1572864 | bytes 8388640 | tf_op jit(solution)/shard_map/sub | solution.py:130
  279.7 2.5 copy.41
  282.2 2.5 copy.42
  284.8 1.9 multiply_add_fusion
  (69 shorter events, 5.0 us)
Async XLA Ops:
  0.6 28.1 %copy-start = (f32[4,32,32,128]{3,2,1,0:T(8,128)S(1)}, f32[4,32,32,128]{3,2,1,0:T(8,128)}, u32[]{:S(2)}) copy-start(f32[4,32,32,128]{3,2,1,0:T(8,128)} %param.16) | copy-start | bytes 6291460
  0.6 26.2 %copy-start.13 = (s32[1,1,4]{2,1,0:T(1,128)S(1)}, s32[1,1,4]{2,1,0:T(1,128)}, u32[]{:S(2)}) copy-start(s32[1,1,4]{2,1,0:T(1,128)} %param.12) | copy-start | bytes 52
  2.5 25.6 %copy-start.11 = (s32[60]{0:T(128)}, s32[60]{0:T(128)S(1)}, u32[]{:S(2)}) copy-start(s32[60]{0:T(128)S(1)} %fusion.36) | copy-start | bytes 724
  4.0 28.0 %all-to-all-start = ((s32[128,2,1]{1,2,0:T(1,128)}), s32[128,2,1]{1,2,0:T(1,128)S(1)}, u32[]{:S(2)}, u32[]{:S(2)}) async-start(s32[128,2,1]{1,2,0:T(1,128)} %bitcast.5), calls=%async_computation | async-start | bytes 131072 | tf_op jit(solution)/shard_map/all_to_all | solution.py:85
  17.1 19.8 %collective-permute-start = (f32[4,1,32,128]{3,1,2,0:T(1,128)}, f32[4,1,32,128]{3,1,2,0:T(1,128)S(1)}, u32[]{:S(2)}, u32[]{:S(2)}) collective-permute-start(f32[4,1,32,128]{3,1,2,0:T(1,128)} %bitcast.16), channel_id=1, source_target_pairs={{16,0},{32,16},{48,32},{64,48},{80,64},{96,80},{112,96},{17,1},{33... | collective-permute-start | bytes 196616 | tf_op jit(solution)/shard_map/ppermute | solution.py:21
  20.0 16.9 %collective-permute-start.1 = (f32[4,1,32,128]{3,1,2,0:T(1,128)}, f32[4,1,32,128]{3,1,2,0:T(1,128)S(1)}, u32[]{:S(2)}, u32[]{:S(2)}) collective-permute-start(f32[4,1,32,128]{3,1,2,0:T(1,128)} %bitcast.17), channel_id=1, source_target_pairs={{0,16},{16,32},{32,48},{48,64},{64,80},{80,96},{96,112},{1,17},{17... | collective-permute-start | bytes 196616 | tf_op jit(solution)/shard_map/ppermute | solution.py:19
  28.7 2.5 copy-start.6
  36.9 5.5 %copy-start.14 = (pred[256]{0:T(512)(128)(4,1)S(1)}, pred[256]{0:T(512)(128)(4,1)}, u32[]{:S(2)}) copy-start(pred[256]{0:T(512)(128)(4,1)} %le.29) | copy-start | bytes 772
  36.9 5.5 %copy-start.15 = (pred[256]{0:T(512)(128)(4,1)S(1)}, pred[256]{0:T(512)(128)(4,1)}, u32[]{:S(2)}) copy-start(pred[256]{0:T(512)(128)(4,1)} %gt.11) | copy-start | bytes 772
  36.9 17.9 %copy-start.10 = (f32[4]{0:T(128)S(1)}, f32[4]{0:T(128)}, u32[]{:S(2)}) copy-start(f32[4]{0:T(128)} %slice_bitcast_fusion) | copy-start | bytes 52
  37.8 16.9 %collective-permute-start.3 = (f32[4,34,1,128]{3,1,2,0:T(8,128)S(1)}, f32[4,34,1,128]{3,1,2,0:T(8,128)S(1)}, u32[]{:S(2)}, u32[]{:S(2)}) collective-permute-start(f32[4,34,1,128]{3,1,2,0:T(8,128)S(1)} %get-tuple-element.42), channel_id=1, source_target_pairs={{0,1},{1,2},{2,3},{3,4},{4,5},{5,6},{6,7},{7,8},{8,9},{9,10},{10,1... | collective-permute-start | bytes 208904 | tf_op jit(solution)/shard_map/ppermute | solution.py:19
  41.1 13.7 %collective-permute-start.2 = (f32[4,34,1,128]{3,1,2,0:T(8,128)S(1)}, f32[4,34,1,128]{3,1,2,0:T(8,128)S(1)}, u32[]{:S(2)}, u32[]{:S(2)}) collective-permute-start(f32[4,34,1,128]{3,1,2,0:T(8,128)S(1)} %get-tuple-element.41), channel_id=1, source_target_pairs={{1,0},{2,1},{3,2},{4,3},{5,4},{6,5},{7,6},{8,7},{9,8},{10,9},{11,1... | collective-permute-start | bytes 208904 | tf_op jit(solution)/shard_map/ppermute | solution.py:21
  44.5 27.1 %all-to-all-start.1 = ((bf16[256,4,128]{2,1,0:T(4,128)(2,1)}), bf16[256,4,128]{2,1,0:T(4,128)(2,1)S(1)}, u32[]{:S(2)}, u32[]{:S(2)}) async-start(bf16[256,4,128]{2,1,0:T(4,128)(2,1)} %select_select_fusion), calls=%async_computation.1 | async-start | bytes 524288 | tf_op jit(solution)/shard_map/all_to_all | solution.py:94
  54.7 17.6 %copy-start.17 = (pred[60]{0:T(512)(128)(4,1)S(1)}, pred[60]{0:T(512)(128)(4,1)}, u32[]{:S(2)}) copy-start(pred[60]{0:T(512)(128)(4,1)} %compare_and_fusion) | copy-start | bytes 184
  64.5 1.3 copy-start.1
  66.0 28.4 %collective-permute-start.4 = (f32[4,1,32,128]{3,1,2,0:T(1,128)S(1)}, f32[4,1,32,128]{3,1,2,0:T(1,128)S(1)}, u32[]{:S(2)}, u32[]{:S(2)}) collective-permute-start(f32[4,1,32,128]{3,1,2,0:T(1,128)S(1)} %get-tuple-element.45), channel_id=1, source_target_pairs={{16,0},{32,16},{48,32},{64,48},{80,64},{96,80},{112,96},{17,1},{33... | collective-permute-start | bytes 196616 | tf_op jit(solution)/shard_map/ppermute | solution.py:21
  68.9 25.5 %collective-permute-start.5 = (f32[4,1,32,128]{3,1,2,0:T(1,128)S(1)}, f32[4,1,32,128]{3,1,2,0:T(1,128)S(1)}, u32[]{:S(2)}, u32[]{:S(2)}) collective-permute-start(f32[4,1,32,128]{3,1,2,0:T(1,128)S(1)} %get-tuple-element.44), channel_id=1, source_target_pairs={{0,16},{16,32},{32,48},{48,64},{64,80},{80,96},{96,112},{1,17},{17... | collective-permute-start | bytes 196616 | tf_op jit(solution)/shard_map/ppermute | solution.py:19
  72.4 3.5 %copy-start.7 = (s32[3]{0:T(128)S(1)}, s32[3]{0:T(128)}, u32[]{:S(2)}) copy-start(s32[3]{0:T(128)} %get-tuple-element.54) | copy-start | bytes 40
  72.4 3.5 %copy-start.8 = (s32[3]{0:T(128)S(1)}, s32[3]{0:T(128)}, u32[]{:S(2)}) copy-start(s32[3]{0:T(128)} %get-tuple-element.55) | copy-start | bytes 40
  72.4 3.5 %copy-start.16 = (pred[3,256]{1,0:T(4,128)(4,1)S(1)}, pred[3,256]{1,0:T(4,128)(4,1)}, u32[]{:S(2)}) copy-start(pred[3,256]{1,0:T(4,128)(4,1)} %add_compare_fusion) | copy-start | bytes 2308
  72.4 4.1 %copy-start.3 = (bf16[1,1,60,256,128]{4,3,2,1,0:T(8,128)(2,1)S(1)}, bf16[1,1,60,256,128]{4,3,2,1,0:T(8,128)(2,1)}, u32[]{:S(2)}) copy-start(bf16[1,1,60,256,128]{4,3,2,1,0:T(8,128)(2,1)} %param.10) | copy-start | bytes 11796484
  76.5 1.5 copy-start.12
  84.9 84.4 %all-to-all-start.2 = ((f32[256,4,128]{2,1,0:T(4,128)}), f32[256,4,128]{2,1,0:T(4,128)S(1)}, u32[]{:S(2)}, u32[]{:S(2)}) async-start(f32[256,4,128]{2,1,0:T(4,128)} %scatter_fusion), calls=%async_computation.2 | async-start | bytes 1048576 | tf_op jit(solution)/shard_map/all_to_all | solution.py:115
  94.4 76.4 %copy-start.9 = (s32[256,1]{0,1:T(1,128)S(1)}, s32[256,1]{0,1:T(1,128)}, u32[]{:S(2)}) copy-start(s32[256,1]{0,1:T(1,128)} %get-tuple-element.49) | copy-start | bytes 3076
  95.3 108.7 %collective-permute-start.7 = (f32[4,34,1,128]{3,1,2,0:T(8,128)S(1)}, f32[4,34,1,128]{3,1,2,0:T(8,128)S(1)}, u32[]{:S(2)}, u32[]{:S(2)}) collective-permute-start(f32[4,34,1,128]{3,1,2,0:T(8,128)S(1)} %get-tuple-element.40), channel_id=1, source_target_pairs={{0,1},{1,2},{2,3},{3,4},{4,5},{5,6},{6,7},{7,8},{8,9},{9,10},{10,1... | collective-permute-start | bytes 208904 | tf_op jit(solution)/shard_map/ppermute | solution.py:19
  98.6 105.4 %collective-permute-start.6 = (f32[4,34,1,128]{3,1,2,0:T(8,128)S(1)}, f32[4,34,1,128]{3,1,2,0:T(8,128)S(1)}, u32[]{:S(2)}, u32[]{:S(2)}) collective-permute-start(f32[4,34,1,128]{3,1,2,0:T(8,128)S(1)} %get-tuple-element.39), channel_id=1, source_target_pairs={{1,0},{2,1},{3,2},{4,3},{5,4},{6,5},{7,6},{8,7},{9,8},{10,9},{11,1... | collective-permute-start | bytes 208904 | tf_op jit(solution)/shard_map/ppermute | solution.py:21
  202.1 2.2 copy-start.2
  210.2 66.5 %copy-start.18 = (f32[3,4]{1,0:T(4,128)S(1)}, f32[3,4]{1,0:T(4,128)}, u32[]{:S(2)}) copy-start(f32[3,4]{1,0:T(4,128)} %param.19) | copy-start | bytes 148
  210.2 66.5 %copy-start.4 = (f32[4,32,32,128]{3,2,1,0:T(8,128)S(1)}, f32[4,32,32,128]{3,2,1,0:T(8,128)}, u32[]{:S(2)}) copy-start(f32[4,32,32,128]{3,2,1,0:T(8,128)} %param.18) | copy-start | bytes 6291460
  282.2 2.5 copy-start.5
where the time goes:
time: 289 us; the launch traced here: 287 us
  blocking collectives  133 us (46%)
  other arithmetic  63.7 us (22%)
  starting transfers between devices  51.4 us (18%)
  local copies, waits for them, and re-layouts  33.1 us (11%)
  matrix products  4.69 us (2%)
    psum x1, blocking collectives, per_device(): residual_sq = lax.psum(residual_sq, ('lat', 'lon'))  68.6 us
    psum x1, blocking collectives, per_device(): lax.psum(jnp.sum(update * update, axis=(1, 2, 3)), ('lat', 'lon'))  63.9 us
    scatter-add x1, other arithmetic, per_device(): jnp.zeros((columns_dev + 1, systems, depth), jnp.float32).at[wanted]  31.4 us
    unnamed x43, local copies, waits for them, and re-layouts  11.9 us
    ppermute x4, starting transfers between devices, with_halo(): lax.ppermute(tail, axis, [(i, (i + 1) % count) for i in range(ends)])  11.7 us
    all_to_all x1, starting transfers between devices, per_device(): lax.all_to_all(request, ('lat', 'lon'), split_axis=0, concat_axis=0, tile...  11.5 us
    all_to_all x1, starting transfers between devices, per_device(): lax.all_to_all(served, ('lat', 'lon'), split_axis=0, concat_axis=0, tiled...  10.2 us
    reduce_sum x1, other arithmetic, per_device(): jnp.sum(damp_bar * damp_bar, axis=(1, 2, 3))  9.79 us
  transfers between devices with their start and end apart: 11, of which 0 were waited for; matrix products, arithmetic and copies ran while one was open for 27% of the time, Pallas kernels for 0%

commit v1 on v0

--- a/solution.py
+++ b/solution.py
@@ -1,11 +1,62 @@
 import jax
 import jax.numpy as jnp
 from jax import lax
+from jax.experimental import pallas as pl
+from jax.experimental.pallas import tpu as pltpu
 from jax.sharding import PartitionSpec as P
 
 DAMP_WEIGHT = 0.15
 EPSILON = 1e-05
 HIGHEST_PRECISION = lax.Precision.HIGHEST
+
+
+MESH = pl.DeviceIdType.MESH
+
+
+def share_kernel(value_ref, all_ref, send_sem, recv_sem):
+    lat_size = lax.axis_size("lat")
+    lon_size = lax.axis_size("lon")
+    devices = lat_size * lon_size
+    me = lax.axis_index("lat") * lon_size + lax.axis_index("lon")
+    barrier = pltpu.get_barrier_semaphore()
+
+    def greet(step, carry):
+        other = lax.rem(me + step, devices)
+        place = (other // lon_size, lax.rem(other, lon_size))
+        pl.semaphore_signal(barrier, inc=1, device_id=place, device_id_type=MESH)
+        return carry
+
+    lax.fori_loop(1, devices, greet, 0)
+    all_ref[me] = value_ref[...]
+    pl.semaphore_wait(barrier, devices - 1)
+
+    def send(step, carry):
+        other = lax.rem(me + step, devices)
+        place = (other // lon_size, lax.rem(other, lon_size))
+        pltpu.make_async_remote_copy(
+            value_ref, all_ref.at[me], send_sem, recv_sem, device_id=place, device_id_type=MESH
+        ).start()
+        return carry
+
+    lax.fori_loop(1, devices, send, 0)
+    most = all_ref.at[pl.ds(0, devices - 1)]
+    pltpu.make_async_copy(most, most, recv_sem).wait()
+    pltpu.make_async_copy(most, most, send_sem).wait()
+
+
+def total(value):
+    devices = lax.axis_size("lat") * lax.axis_size("lon")
+    wide = jnp.pad(value[None], ((0, 0), (0, 128 - value.shape[0])))
+    gathered = pl.pallas_call(
+        share_kernel,
+        out_shape=jax.ShapeDtypeStruct((devices, 1, 128), jnp.float32),
+        in_specs=[pl.BlockSpec(memory_space=pltpu.VMEM)],
+        out_specs=pl.BlockSpec(memory_space=pltpu.VMEM),
+        scratch_shapes=[pltpu.SemaphoreType.DMA, pltpu.SemaphoreType.DMA],
+        compiler_params=pltpu.CompilerParams(collective_id=0, has_side_effects=True),
+        name="share",
+    )(wide)
+    return jnp.sum(gathered[:, 0, : value.shape[0]], axis=0)
 
 
 def with_halo(cells, sides, width):
@@ -116,11 +167,11 @@
     collected = jnp.zeros((columns_dev + 1, systems, depth), jnp.float32).at[wanted].add(incoming)
     remote_part = collected[1:].reshape(clat_dev, clon_dev, systems, depth).transpose(2, 0, 1, 3)
     adjoint_image = remote_part + DAMP_WEIGHT * laplace(damp_bar)
-    residual_sq = lax.psum(residual_sq, ("lat", "lon"))
+    residual_sq = total(residual_sq)
     beta_new = jnp.sqrt(residual_sq / rows_all + EPSILON)
     beta_wide = beta_new[:, None, None, None]
     update = adjoint_image / beta_wide - beta_wide * model_vector
-    update_sq = lax.psum(jnp.sum(update * update, axis=(1, 2, 3)), ("lat", "lon"))
+    update_sq = total(jnp.sum(update * update, axis=(1, 2, 3)))
     alpha_new = jnp.sqrt(update_sq / cells_all + EPSILON)
     model_out = update / alpha_new[:, None, None, None]
     rho_new = jnp.sqrt(rho_bar * rho_bar + beta_new * beta_new)

time: 289 us -> 201 us (0.70)
  blocking collectives: 133 us -> 0 us
  Pallas kernels: 0 us -> 33.5 us
  waiting for transfers between devices: 0.03 us -> 13.7 us
  starting transfers between devices: 51.4 us -> 47.6 us
    psum x2 -> x0, blocking collectives: 133 us -> none  [the longest x1 68.6 us: per_device(): residual_sq = lax.psum(residual_sq, ('lat', 'lon'))]
    pallas_call x0 -> x2, Pallas kernels: none -> 33.5 us  [total(): pl.pallas_call(share_kernel, out_shape=jax.ShapeDtypeStruct((devices, 1,...]
    all_to_all x1, waiting for transfers between devices: 0.01 us -> 12.4 us  [per_device(): lax.all_to_all(outgoing, ('lat', 'lon'), split_axis=0, concat_axis=0, til...]
    all_to_all x1, starting transfers between devices: 9.47 us -> 5.63 us  [per_device(): lax.all_to_all(outgoing, ('lat', 'lon'), split_axis=0, concat_axis=0, til...]
    reduce_sum x1 -> x3, other arithmetic: 5.86 us -> 6.39 us  [the longest x1 5.25 us: per_device(): update_sq = total(jnp.sum(update * update, axis=(1, 2, 3)))]
  transfers between devices with their start and end apart: 11 -> 11, of which waited for: 0 -> 2; matrix products, arithmetic and copies ran while one was open for 27% -> 39% of each run, Pallas kernels for 0% -> 10%
where the time goes in v1:
time: 201 us; the launch traced here: 199 us
  other arithmetic  61.5 us (31%)
  starting transfers between devices  47.6 us (24%)
  local copies, waits for them, and re-layouts  34.6 us (17%)
  Pallas kernels  33.5 us (17%)
  waiting for transfers between devices  13.7 us (7%)
  matrix products  6.68 us (3%)
    pallas_call x2, Pallas kernels, total(): pl.pallas_call(share_kernel, out_shape=jax.ShapeDtypeStruct((devices, 1,...  33.5 us
    scatter-add x1, other arithmetic, per_device(): jnp.zeros((columns_dev + 1, systems, depth), jnp.float32).at[wanted]  31.7 us
    all_to_all x1, waiting for transfers between devices, per_device(): lax.all_to_all(outgoing, ('lat', 'lon'), split_axis=0, concat_axis=0, til...  12.4 us
    unnamed x43, local copies, waits for them, and re-layouts  12.3 us
    ppermute x4, starting transfers between devices, with_halo(): lax.ppermute(tail, axis, [(i, (i + 1) % count) for i in range(ends)])  11.7 us
    all_to_all x1, starting transfers between devices, per_device(): lax.all_to_all(request, ('lat', 'lon'), split_axis=0, concat_axis=0, tile...  11.5 us
    all_to_all x1, starting transfers between devices, per_device(): lax.all_to_all(served, ('lat', 'lon'), split_axis=0, concat_axis=0, tiled...  10.2 us
    reduce_sum x1, other arithmetic, per_device(): jnp.sum(damp_bar * damp_bar, axis=(1, 2, 3))  9.79 us
  transfers between devices with their start and end apart: 11, of which 2 were waited for; matrix products, arithmetic and copies ran while one was open for 39% of the time, Pallas kernels for 10%

profile of v1, /device:TPU:1, one launch (start us, length us, event | category | flops | bytes accessed | tf_op | source)
XLA Modules:
  0.0 199.3 jit_solution(14600635807854168893)
XLA Ops:
  0.7 0.8 fusion.42
  1.8 0.7 fusion.36
  2.5 0.8 scatter_custom_fusion
  3.3 0.8 all_to_all.14
  4.0 11.5 %all-to-all-start = ((s32[128,2,1]{1,2,0:T(1,128)}), s32[128,2,1]{1,2,0:T(1,128)S(1)}, u32[]{:S(2)}, u32[]{:S(2)}) async-start(s32[128,2,1]{1,2,0:T(1,128)} %bitcast.5), calls=%async_computation | async-start | bytes 131072 | tf_op jit(solution)/shard_map/all_to_all | solution.py:136
  15.5 1.5 fusion.53
  17.1 3.0 %collective-permute-start = (f32[4,1,32,128]{3,1,2,0:T(1,128)}, f32[4,1,32,128]{3,1,2,0:T(1,128)S(1)}, u32[]{:S(2)}, u32[]{:S(2)}) collective-permute-start(f32[4,1,32,128]{3,1,2,0:T(1,128)} %bitcast.16), channel_id=1, source_target_pairs={{16,0},{32,16},{48,32},{64,48},{80,64},{96,80},{112,96},{17,1},{33... | collective-permute-start | bytes 196616 | tf_op jit(solution)/shard_map/ppermute | solution.py:72
  20.0 2.6 %collective-permute-start.1 = (f32[4,1,32,128]{3,1,2,0:T(1,128)}, f32[4,1,32,128]{3,1,2,0:T(1,128)S(1)}, u32[]{:S(2)}, u32[]{:S(2)}) collective-permute-start(f32[4,1,32,128]{3,1,2,0:T(1,128)} %bitcast.17), channel_id=1, source_target_pairs={{0,16},{16,32},{32,48},{48,64},{64,80},{80,96},{96,112},{1,17},{17... | collective-permute-start | bytes 196616 | tf_op jit(solution)/shard_map/ppermute | solution.py:70
  22.6 1.8 convert_bitcast_fusion
  25.0 1.2 slice_bitcast_fusion
  26.2 0.6 slice_bitcast_fusion.2
  27.4 2.5 %copy.27 = f32[4,32,32,128]{3,1,2,0:T(8,128)} copy(f32[4,32,32,128]{3,2,1,0:T(8,128)S(1)} %copy-done) | data formatting | bytes 4194304 | tf_op args[6]
  30.0 0.8 copy.23
  32.0 0.8 reduce.9
  34.0 0.7 le.29
  34.6 0.7 gt.11
  35.3 1.0 gather_fusion
  36.3 0.9 pad_maximum_fusion.21
  37.2 3.2 %collective-permute-start.3 = (f32[4,34,1,128]{3,1,2,0:T(8,128)S(1)}, f32[4,34,1,128]{3,1,2,0:T(8,128)S(1)}, u32[]{:S(2)}, u32[]{:S(2)}) collective-permute-start(f32[4,34,1,128]{3,1,2,0:T(8,128)S(1)} %get-tuple-element.37), channel_id=1, source_target_pairs={{0,1},{1,2},{2,3},{3,4},{4,5},{5,6},{6,7},{7,8},{8,9},{9,10},{10,1... | collective-permute-start | bytes 208904 | tf_op jit(solution)/shard_map/ppermute | solution.py:70
  40.5 1.3 collective-permute-start.2
  41.8 2.1 %select_select_fusion = bf16[256,4,128]{2,1,0:T(4,128)(2,1)} fusion(bf16[256,4,128]{2,1,0:T(4,128)(2,1)S(1)} %gather_fusion, pred[256]{0:T(512)(128)(4,1)S(1)} %copy-done.16, pred[256]{0:T(512)(128)(4,1)S(1)} %copy-done.17), kind=kLoop, calls=%fused_computation.61 | loop fusion | flops 262144 | bytes 524800 | tf_op jit(solution)/shard_map/jit(_where)/select_n | solution.py:140
  43.9 10.2 %all-to-all-start.1 = ((bf16[256,4,128]{2,1,0:T(4,128)(2,1)}), bf16[256,4,128]{2,1,0:T(4,128)(2,1)S(1)}, u32[]{:S(2)}, u32[]{:S(2)}) async-start(bf16[256,4,128]{2,1,0:T(4,128)(2,1)} %select_select_fusion), calls=%async_computation.1 | async-start | bytes 524288 | tf_op jit(solution)/shard_map/all_to_all | solution.py:145
  54.2 9.8 %multiply_reduce_fusion.1 = (f32[4]{0:T(128)S(1)}, f32[4,32,32,128]{3,1,2,0:T(8,128)S(1)}) fusion(f32[4,32,32,128]{3,2,1,0:T(8,128)} %param.15, f32[4]{0:T(128)S(1)} %copy-done.11, f32[4,32,32,128]{3,1,2,0:T(8,128)} %copy.27, f32[4,1,32,128]{3,1,2,0:T(1,128)S(1)} %collective-permute-done, f32[4,1,32,128]{3,1,2,0:T(1,128)S(1)} %collective-permute-done.1, ...), kind=kLoop, calls=%fused_computation.52 | loop fusion | flops 10485756 | bytes 6561824 | tf_op jit(solution)/shard_map/reduce_sum | solution.py:155
  64.1 3.0 %collective-permute-start.4 = (f32[4,1,32,128]{3,1,2,0:T(1,128)S(1)}, f32[4,1,32,128]{3,1,2,0:T(1,128)S(1)}, u32[]{:S(2)}, u32[]{:S(2)}) collective-permute-start(f32[4,1,32,128]{3,1,2,0:T(1,128)S(1)} %get-tuple-element.40), channel_id=1, source_target_pairs={{16,0},{32,16},{48,32},{64,48},{80,64},{96,80},{112,96},{17,1},{33... | collective-permute-start | bytes 196616 | tf_op jit(solution)/shard_map/ppermute | solution.py:72
  67.1 2.6 %collective-permute-start.5 = (f32[4,1,32,128]{3,1,2,0:T(1,128)S(1)}, f32[4,1,32,128]{3,1,2,0:T(1,128)S(1)}, u32[]{:S(2)}, u32[]{:S(2)}) collective-permute-start(f32[4,1,32,128]{3,1,2,0:T(1,128)S(1)} %get-tuple-element.39), channel_id=1, source_target_pairs={{0,16},{16,32},{32,48},{48,64},{64,80},{80,96},{96,112},{1,17},{17... | collective-permute-start | bytes 196616 | tf_op jit(solution)/shard_map/ppermute | solution.py:70
  69.7 1.3 collective-permute-done.5
  71.0 3.2 %collective-permute-start.7 = (f32[4,34,1,128]{3,1,2,0:T(8,128)S(1)}, f32[4,34,1,128]{3,1,2,0:T(8,128)S(1)}, u32[]{:S(2)}, u32[]{:S(2)}) collective-permute-start(f32[4,34,1,128]{3,1,2,0:T(8,128)S(1)} %get-tuple-element.35), channel_id=1, source_target_pairs={{0,1},{1,2},{2,3},{3,4},{4,5},{5,6},{6,7},{7,8},{8,9},{9,10},{10,1... | collective-permute-start | bytes 208904 | tf_op jit(solution)/shard_map/ppermute | solution.py:70
  74.3 1.3 collective-permute-start.6
  75.6 0.8 gather_fusion.1
  76.4 3.3 %fusion.2 = f32[60,4,256]{2,1,0:T(4,128)S(1)} fusion(bf16[1,1,60,256,128]{4,3,2,1,0:T(8,128)(2,1)} %param.10, bf16[60,4,128]{2,1,0:T(4,128)(2,1)S(1)} %gather_fusion.1, pred[60]{0:T(512)(128)(4,1)S(1)} %copy-done.18), kind=kOutput, calls=%fused_computation.11 | convolution fusion | flops 15759360 | bytes 4239420 | tf_op jit(solution)/shard_map/tid,trd->tri/dot_general | solution.py:148
  80.6 20.1 %share.2 = f32[128,1,128]{2,1,0:T(1,128)} custom-call(f32[1,128]{1,0:T(1,128)} %pad.15.value_ref), custom_call_target="tpu_custom_call" | custom-call | tf_op jit(solution)/shard_map/share/pallas_call | solution.py:50
  101.0 2.8 %fusion = f32[60,4,128]{2,1,0:T(4,128)S(1)} fusion(bf16[1,1,60,256,128]{4,3,2,1,0:T(8,128)(2,1)} %param.10, bf16[60,4,256]{2,0,1:T(8,128)(2,1)S(1)} %convolution_convert_fusion), kind=kOutput, calls=%fused_computation.9 | convolution fusion | flops 15728640 | bytes 4177920 | tf_op jit(solution)/shard_map/tid,tri->trd/dot_general | solution.py:162
  103.8 0.9 broadcast_in_dim.78
  104.6 6.9 %scatter_fusion = f32[256,4,128]{2,1,0:T(4,128)} fusion(f32[256,4,128]{2,1,0:T(4,128)} %broadcast_in_dim.78, s32[60]{0:T(128)S(1)} %copy-done.13, f32[60,4,128]{2,1,0:T(4,128)S(1)} %fusion), kind=kCustom, calls=%fused_computation.3 | custom fusion | bytes 368880 | tf_op jit(solution)/shard_map/scatter | solution.py:164
  111.5 5.6 %all-to-all-start.2 = ((f32[256,4,128]{2,1,0:T(4,128)}), f32[256,4,128]{2,1,0:T(4,128)S(1)}, u32[]{:S(2)}, u32[]{:S(2)}) async-start(f32[256,4,128]{2,1,0:T(4,128)} %scatter_fusion), calls=%async_computation.2 | async-start | bytes 1048576 | tf_op jit(solution)/shard_map/all_to_all | solution.py:166
  117.4 0.6 reshape.363
  118.0 12.4 %all-to-all-done.2 = f32[256,4,128]{2,1,0:T(4,128)S(1)} async-done(((f32[256,4,128]{2,1,0:T(4,128)}), f32[256,4,128]{2,1,0:T(4,128)S(1)}, u32[]{:S(2)}, u32[]{:S(2)}) %all-to-all-start.2) | async-done | bytes 524320 | tf_op jit(solution)/shard_map/all_to_all | solution.py:166
  130.5 1.5 broadcast_in_dim.77
  132.0 31.7 %scatter_fusion.1 = f32[1025,4,128]{2,1,0:T(4,128)} fusion(f32[1025,4,128]{2,1,0:T(4,128)} %broadcast_in_dim.77, s32[256]{0:T(256)S(1)} %bitcast.109, f32[256,4,128]{2,1,0:T(4,128)S(1)} %all-to-all-done.2), kind=kCustom, calls=%fused_computation.4 | custom fusion | flops 131072 | bytes 1573888 | tf_op jit(solution)/shard_map/scatter-add | solution.py:167
  163.7 1.9 slice.126
  165.9 5.2 %multiply_reduce_fusion = (f32[4]{0:T(128)S(1)}, f32[4,32,32,128]{3,1,2,0:T(8,128)}, f32[4,32,32,128]{3,1,2,0:T(8,128)}) fusion(f32[4,32,32,128]{3,2,1,0:T(8,128)S(1)} %copy-done, f32[4]{0:T(128)S(1)} %add_sqrt_fusion.1, f32[4,32,32,128]{3,1,2,0:T(8,128)S(1)} %copy-done.2, f32[4,1,32,128]{3,1,2,0:T(1,128)S(1)} %collective-permute-done.4, ...), kind=kLoop, calls=%fused_computation.51 | loop fusion | flops 12058620 | bytes 10756128 | tf_op jit(solution)/shard_map/reduce_sum | solution.py:174
  171.6 13.4 %share.3 = f32[128,1,128]{2,1,0:T(1,128)} custom-call(f32[1,128]{1,0:T(1,128)} %pad.17.value_ref), custom_call_target="tpu_custom_call" | custom-call | tf_op jit(solution)/shard_map/share/pallas_call | solution.py:50
  185.1 1.0 slice_reduce_fusion
  186.1 4.3 %copy.40 = f32[4,32,32,128]{3,2,1,0:T(8,128)} copy(f32[4,32,32,128]{3,1,2,0:T(8,128)} %get-tuple-element.38) | data formatting | bytes 4194304
  190.4 1.3 fusion.22
  191.8 2.5 %copy.41 = f32[4,32,32,128]{3,2,1,0:T(8,128)} copy(f32[4,32,32,128]{3,1,2,0:T(8,128)S(1)} %get-tuple-element.27) | data formatting | bytes 4194304
  194.3 2.5 %copy.42 = f32[4,32,32,128]{3,2,1,0:T(8,128)} copy(f32[4,32,32,128]{3,1,2,0:T(8,128)S(1)} %get-tuple-element.26) | data formatting | bytes 4194304
  196.8 1.9 multiply_add_fusion
  (72 shorter events, 6.3 us)
Async XLA Ops:
  0.6 26.8 %copy-start = (f32[4,32,32,128]{3,2,1,0:T(8,128)S(1)}, f32[4,32,32,128]{3,2,1,0:T(8,128)}, u32[]{:S(2)}) copy-start(f32[4,32,32,128]{3,2,1,0:T(8,128)} %param.16) | copy-start | bytes 6291460
  0.6 25.6 %copy-start.15 = (s32[1,1,4]{2,1,0:T(1,128)S(1)}, s32[1,1,4]{2,1,0:T(1,128)}, u32[]{:S(2)}) copy-start(s32[1,1,4]{2,1,0:T(1,128)} %param.12) | copy-start | bytes 52
  2.5 24.3 %copy-start.12 = (s32[60]{0:T(128)}, s32[60]{0:T(128)S(1)}, u32[]{:S(2)}) copy-start(s32[60]{0:T(128)S(1)} %fusion.36) | copy-start | bytes 724
  4.0 27.4 %all-to-all-start = ((s32[128,2,1]{1,2,0:T(1,128)}), s32[128,2,1]{1,2,0:T(1,128)S(1)}, u32[]{:S(2)}, u32[]{:S(2)}) async-start(s32[128,2,1]{1,2,0:T(1,128)} %bitcast.5), calls=%async_computation | async-start | bytes 131072 | tf_op jit(solution)/shard_map/all_to_all | solution.py:136
  17.1 19.3 %collective-permute-start = (f32[4,1,32,128]{3,1,2,0:T(1,128)}, f32[4,1,32,128]{3,1,2,0:T(1,128)S(1)}, u32[]{:S(2)}, u32[]{:S(2)}) collective-permute-start(f32[4,1,32,128]{3,1,2,0:T(1,128)} %bitcast.16), channel_id=1, source_target_pairs={{16,0},{32,16},{48,32},{64,48},{80,64},{96,80},{112,96},{17,1},{33... | collective-permute-start | bytes 196616 | tf_op jit(solution)/shard_map/ppermute | solution.py:72
  20.0 16.3 %collective-permute-start.1 = (f32[4,1,32,128]{3,1,2,0:T(1,128)}, f32[4,1,32,128]{3,1,2,0:T(1,128)S(1)}, u32[]{:S(2)}, u32[]{:S(2)}) collective-permute-start(f32[4,1,32,128]{3,1,2,0:T(1,128)} %bitcast.17), channel_id=1, source_target_pairs={{0,16},{16,32},{32,48},{48,64},{64,80},{80,96},{96,112},{1,17},{17... | collective-permute-start | bytes 196616 | tf_op jit(solution)/shard_map/ppermute | solution.py:70
  27.4 2.5 %copy-start.7 = (f32[4,1,1,768]{3,2,1,0:T(1,128)S(1)}, f32[4,1,1,768]{3,2,1,0:T(1,128)}, u32[]{:S(2)}) copy-start(f32[4,1,1,768]{3,2,1,0:T(1,128)} %param.14) | copy-start | bytes 36868
  36.3 5.5 %copy-start.16 = (pred[256]{0:T(512)(128)(4,1)S(1)}, pred[256]{0:T(512)(128)(4,1)}, u32[]{:S(2)}) copy-start(pred[256]{0:T(512)(128)(4,1)} %le.29) | copy-start | bytes 772
  36.3 5.5 %copy-start.17 = (pred[256]{0:T(512)(128)(4,1)S(1)}, pred[256]{0:T(512)(128)(4,1)}, u32[]{:S(2)}) copy-start(pred[256]{0:T(512)(128)(4,1)} %gt.11) | copy-start | bytes 772
  36.3 17.9 %copy-start.11 = (f32[4]{0:T(128)S(1)}, f32[4]{0:T(128)}, u32[]{:S(2)}) copy-start(f32[4]{0:T(128)} %slice_bitcast_fusion) | copy-start | bytes 52
  37.2 16.9 %collective-permute-start.3 = (f32[4,34,1,128]{3,1,2,0:T(8,128)S(1)}, f32[4,34,1,128]{3,1,2,0:T(8,128)S(1)}, u32[]{:S(2)}, u32[]{:S(2)}) collective-permute-start(f32[4,34,1,128]{3,1,2,0:T(8,128)S(1)} %get-tuple-element.37), channel_id=1, source_target_pairs={{0,1},{1,2},{2,3},{3,4},{4,5},{5,6},{6,7},{7,8},{8,9},{9,10},{10,1... | collective-permute-start | bytes 208904 | tf_op jit(solution)/shard_map/ppermute | solution.py:70
  40.5 13.7 %collective-permute-start.2 = (f32[4,34,1,128]{3,1,2,0:T(8,128)S(1)}, f32[4,34,1,128]{3,1,2,0:T(8,128)S(1)}, u32[]{:S(2)}, u32[]{:S(2)}) collective-permute-start(f32[4,34,1,128]{3,1,2,0:T(8,128)S(1)} %get-tuple-element.36), channel_id=1, source_target_pairs={{1,0},{2,1},{3,2},{4,3},{5,4},{6,5},{7,6},{8,7},{9,8},{10,9},{11,1... | collective-permute-start | bytes 208904 | tf_op jit(solution)/shard_map/ppermute | solution.py:72
  43.9 31.7 %all-to-all-start.1 = ((bf16[256,4,128]{2,1,0:T(4,128)(2,1)}), bf16[256,4,128]{2,1,0:T(4,128)(2,1)S(1)}, u32[]{:S(2)}, u32[]{:S(2)}) async-start(bf16[256,4,128]{2,1,0:T(4,128)(2,1)} %select_select_fusion), calls=%async_computation.1 | async-start | bytes 524288 | tf_op jit(solution)/shard_map/all_to_all | solution.py:145
  64.0 7.0 %copy-start.1 = (f32[4,32,32,128]{3,1,2,0:T(8,128)}, f32[4,32,32,128]{3,1,2,0:T(8,128)S(1)}, u32[]{:S(2)}) copy-start(f32[4,32,32,128]{3,1,2,0:T(8,128)S(1)} %get-tuple-element.31) | copy-start | bytes 6291460
  64.0 12.4 %copy-start.18 = (pred[60]{0:T(512)(128)(4,1)S(1)}, pred[60]{0:T(512)(128)(4,1)}, u32[]{:S(2)}) copy-start(pred[60]{0:T(512)(128)(4,1)} %compare_and_fusion) | copy-start | bytes 184
  64.1 5.6 %collective-permute-start.4 = (f32[4,1,32,128]{3,1,2,0:T(1,128)S(1)}, f32[4,1,32,128]{3,1,2,0:T(1,128)S(1)}, u32[]{:S(2)}, u32[]{:S(2)}) collective-permute-start(f32[4,1,32,128]{3,1,2,0:T(1,128)S(1)} %get-tuple-element.40), channel_id=1, source_target_pairs={{16,0},{32,16},{48,32},{64,48},{80,64},{96,80},{112,96},{17,1},{33... | collective-permute-start | bytes 196616 | tf_op jit(solution)/shard_map/ppermute | solution.py:72
  67.1 3.9 %collective-permute-start.5 = (f32[4,1,32,128]{3,1,2,0:T(1,128)S(1)}, f32[4,1,32,128]{3,1,2,0:T(1,128)S(1)}, u32[]{:S(2)}, u32[]{:S(2)}) collective-permute-start(f32[4,1,32,128]{3,1,2,0:T(1,128)S(1)} %get-tuple-element.39), channel_id=1, source_target_pairs={{0,16},{16,32},{32,48},{48,64},{64,80},{80,96},{96,112},{1,17},{17... | collective-permute-start | bytes 196616 | tf_op jit(solution)/shard_map/ppermute | solution.py:70
  71.0 94.5 %collective-permute-start.7 = (f32[4,34,1,128]{3,1,2,0:T(8,128)S(1)}, f32[4,34,1,128]{3,1,2,0:T(8,128)S(1)}, u32[]{:S(2)}, u32[]{:S(2)}) collective-permute-start(f32[4,34,1,128]{3,1,2,0:T(8,128)S(1)} %get-tuple-element.35), channel_id=1, source_target_pairs={{0,1},{1,2},{2,3},{3,4},{4,5},{5,6},{6,7},{7,8},{8,9},{9,10},{10,1... | collective-permute-start | bytes 208904 | tf_op jit(solution)/shard_map/ppermute | solution.py:70
  74.3 91.3 %collective-permute-start.6 = (f32[4,34,1,128]{3,1,2,0:T(8,128)S(1)}, f32[4,34,1,128]{3,1,2,0:T(8,128)S(1)}, u32[]{:S(2)}, u32[]{:S(2)}) collective-permute-start(f32[4,34,1,128]{3,1,2,0:T(8,128)S(1)} %get-tuple-element.34), channel_id=1, source_target_pairs={{1,0},{2,1},{3,2},{4,3},{5,4},{6,5},{7,6},{8,7},{9,8},{10,9},{11,1... | collective-permute-start | bytes 208904 | tf_op jit(solution)/shard_map/ppermute | solution.py:72
  76.4 3.3 %copy-start.8 = (s32[3]{0:T(128)S(1)}, s32[3]{0:T(128)}, u32[]{:S(2)}) copy-start(s32[3]{0:T(128)} %get-tuple-element.51) | copy-start | bytes 40
  76.4 3.3 %copy-start.9 = (s32[3]{0:T(128)S(1)}, s32[3]{0:T(128)}, u32[]{:S(2)}) copy-start(s32[3]{0:T(128)} %get-tuple-element.52) | copy-start | bytes 40
  101.0 3.7 %copy-start.13 = (s32[60]{0:T(128)S(1)}, s32[60]{0:T(128)}, u32[]{:S(2)}) copy-start(s32[60]{0:T(128)} %copy-done.12) | copy-start | bytes 724
  101.0 16.2 %copy-start.6 = (f32[128,1,128]{2,1,0:T(1,128)S(1)}, f32[128,1,128]{2,1,0:T(1,128)}, u32[]{:S(2)}) copy-start(f32[128,1,128]{2,1,0:T(1,128)} %share.2) | copy-start | bytes 196612
  103.7 28.2 %copy-start.10 = (s32[256,1]{0,1:T(1,128)S(1)}, s32[256,1]{0,1:T(1,128)}, u32[]{:S(2)}) copy-start(s32[256,1]{0,1:T(1,128)} %get-tuple-element.47) | copy-start | bytes 3076
  111.5 19.0 %all-to-all-start.2 = ((f32[256,4,128]{2,1,0:T(4,128)}), f32[256,4,128]{2,1,0:T(4,128)S(1)}, u32[]{:S(2)}, u32[]{:S(2)}) async-start(f32[256,4,128]{2,1,0:T(4,128)} %scatter_fusion), calls=%async_computation.2 | async-start | bytes 1048576 | tf_op jit(solution)/shard_map/all_to_all | solution.py:166
  163.7 2.2 %copy-start.2 = (f32[4,32,32,128]{3,1,2,0:T(8,128)S(1)}, f32[4,32,32,128]{3,1,2,0:T(8,128)}, u32[]{:S(2)}) copy-start(f32[4,32,32,128]{3,1,2,0:T(8,128)} %copy-done.1) | copy-start | bytes 6291460
  165.9 20.2 %copy-start.14 = (f32[3,4]{1,0:T(4,128)S(1)}, f32[3,4]{1,0:T(4,128)}, u32[]{:S(2)}) copy-start(f32[3,4]{1,0:T(4,128)} %param.19) | copy-start | bytes 148
  186.1 4.3 %copy-start.3 = (f32[4,32,32,128]{3,2,1,0:T(8,128)S(1)}, f32[4,32,32,128]{3,2,1,0:T(8,128)}, u32[]{:S(2)}) copy-start(f32[4,32,32,128]{3,2,1,0:T(8,128)} %param.18) | copy-start | bytes 6291460
  186.1 4.3 %copy-start.4 = (f32[4,32,32,128]{3,1,2,0:T(8,128)S(1)}, f32[4,32,32,128]{3,1,2,0:T(8,128)}, u32[]{:S(2)}) copy-start(f32[4,32,32,128]{3,1,2,0:T(8,128)} %get-tuple-element.29) | copy-start | bytes 6291460
  194.3 2.5 %copy-start.5 = (f32[4,32,32,128]{3,2,1,0:T(8,128)S(1)}, f32[4,32,32,128]{3,2,1,0:T(8,128)}, u32[]{:S(2)}) copy-start(f32[4,32,32,128]{3,2,1,0:T(8,128)} %param.17) | copy-start | bytes 6291460

commit v2 on v0

v2 whole, which is shorter than its diff:
```python
import jax
import jax.numpy as jnp
from jax import lax
from jax.experimental import pallas as pl
from jax.experimental.pallas import tpu as pltpu
from jax.sharding import PartitionSpec as P

DAMP_WEIGHT = 0.15
EPSILON = 1e-05
MESH = pl.DeviceIdType.MESH
F32 = jnp.float32
BF16 = jnp.bfloat16

R = 4
CLAT = 32
CLON = 32
DEPTH = 128
BLK = CLAT * CLON
TILES = 60
RAYS_BLK = 256
RBMAX = 3
N_LAT = 8
N_LON = 16
NDEV = N_LAT * N_LON
LAT_PAD = CLAT + 2
LON_PAD = CLON + 16
LEFT = 8
ROWS_ALL = NDEV * RBMAX * RAYS_BLK + NDEV * BLK * DEPTH
CELLS = NDEV * BLK * DEPTH
INNER = pl.ds(LEFT, CLON)


def iota(shape, axis):
    return lax.broadcasted_iota(jnp.int32, shape, axis)


def one(cond):
    return jnp.where(cond, 1.0, 0.0)


def dot(a, b):
    return jnp.dot(a, b, preferred_element_type=F32)


def laplace_slab(ref, r, row):
    here = ref[r, row + 1, INNER]
    beside = ref[r, row, INNER] + ref[r, row + 2, INNER]
    beside = beside + ref[r, row + 1, pl.ds(LEFT - 1, CLON)] + ref[r, row + 1, pl.ds(LEFT + 1, CLON)]
    lane = iota((CLON, DEPTH), 1)
    above = jnp.where(lane == 0, 0.0, pltpu.roll(here, 1, 1))
    below = jnp.where(lane == DEPTH - 1, 0.0, pltpu.roll(here, DEPTH - 1, 1))
    return 6.0 * here - (beside + above + below)


def fold(x):
    return x[0:8] + x[8:16] + x[16:24] + x[24:32]


def step_kernel(
    ids_s, off_s, cnt_s, rec_s, ids_v, rec_v, ray_v, sens_h, damp_h, model_h, sol_h, search_h,
    upd_o, damp_o, sol_o, search_o, coef_o, ray_o, rec_o,
    mp, dp, dv, sens, idrow, ids_all, idcol, slotcol, rowval, sel, selt, oh, oht,
    resp, fetched, wts, terms, outg, inc, zbuf, sum_a, sums_a, sum_b, sums_b,
    edge_s, edge_r, row_r, ray_keep,
    load_sem, send_sem, recv_sem, edge_ssem, edge_rsem,
):
    my_lat = lax.axis_index("lat")
    my_lon = lax.axis_index("lon")
    me = my_lat * N_LON + my_lon

    def place(other):
        return (other // N_LON, lax.rem(other, N_LON))

    barrier = pltpu.get_barrier_semaphore()

    def greet(step, carry):
        other = lax.rem(me + step, NDEV)
        pl.semaphore_signal(barrier, inc=1, device_id=place(other), device_id_type=MESH)
        return carry

    lax.fori_loop(1, NDEV, greet, 0)

    loads = [
        pltpu.make_async_copy(model_h, mp.at[:, pl.ds(1, CLAT), INNER, :], load_sem.at[0]),
        pltpu.make_async_copy(damp_h, dv, load_sem.at[1]),
        pltpu.make_async_copy(sens_h, sens, load_sem.at[2]),
        pltpu.make_async_copy(sol_h, sol_o, load_sem.at[3]),
        pltpu.make_async_copy(search_h, search_o, load_sem.at[4]),
    ]
    for load in loads:
        load.start()

    idrow[...] = jnp.full((1, 128), -1, jnp.int32)
    idrow[:, 0:TILES] = ids_v[...]

    side = jnp.zeros((R, LAT_PAD, LEFT, DEPTH), F32)
    mp[:, :, pl.ds(0, LEFT), :] = side
    mp[:, :, pl.ds(LEFT + CLON, LEFT), :] = side
    dp[:, :, pl.ds(0, LEFT), :] = side
    dp[:, :, pl.ds(LEFT + CLON, LEFT), :] = side
    flat = jnp.zeros((R, CLON, DEPTH), F32)

    @pl.when(my_lat == 0)
    def _():
        mp[:, 0, INNER, :] = flat
        dp[:, 0, INNER, :] = flat

    @pl.when(my_lat == N_LAT - 1)
    def _():
        mp[:, LAT_PAD - 1, INNER, :] = flat
        dp[:, LAT_PAD - 1, INNER, :] = flat

    for t in range(TILES):
        idcol[t : t + 1, :] = jnp.full((1, 128), ids_s[0, t], jnp.int32)
    idcol[TILES:64, :] = jnp.full((64 - TILES, 128), -1, jnp.int32)
    owner_col = idcol[...] >> 10
    owner_row = jnp.broadcast_to(idrow[...] >> 10, (64, 128))
    twin = one((owner_col == owner_row) & (iota((64, 128), 1) < iota((64, 128), 0)))
    rank = jnp.max(twin, axis=1, keepdims=True).astype(jnp.int32)
    slotcol[...] = jnp.where(iota((64, 128), 0) < TILES, (owner_col * 2 + rank) * 4, -64)

    row16 = iota((16, 128), 0)
    blk16 = row16 // 4
    first16 = jnp.where(blk16 == 0, off_s[0, 0], jnp.where(blk16 == 1, off_s[0, 1], off_s[0, 2]))
    last16 = jnp.where(
        blk16 == 0, off_s[0, 1],
        jnp.where(blk16 == 1, off_s[0, 2], jnp.where(blk16 == 2, off_s[0, 3], 0)),
    )
    lane16 = iota((16, 128), 1)

    def build_sel(t, carry):
        slot = jnp.broadcast_to(slotcol[pl.ds(t, 1), :], (16, 128))
        value = jnp.where((first16 <= t) & (t < last16), slot + (row16 & 3), -1)
        rows = pl.ds(pl.multiple_of(t * 16, 16), 16)
        rowval[rows, :] = value.astype(F32)
        for j in range(8):
            sel[rows, j * 128 : (j + 1) * 128] = one(value == lane16 + j * 128).astype(BF16)
        return carry

    lax.fori_loop(0, 64, build_sel, 0, unroll=2)

    pl.semaphore_wait(barrier, NDEV - 1)

    def share(src, dst, k):
        def send(step, carry):
            other = lax.rem(me + step, NDEV)
            pltpu.make_async_remote_copy(
                src, dst.at[me], send_sem.at[k], recv_sem.at[k],
                device_id=place(other), device_id_type=MESH,
            ).start()
            return carry

        lax.fori_loop(1, NDEV, send, 0)
        dst[me] = src[...]

    def settle(dst, sem):
        most = dst.at[pl.ds(0, NDEV - 1)]
        pltpu.make_async_copy(most, most, sem).wait()

    share(idrow, ids_all, 0)

    def edge(buf, k, base):
        n = base + k
        if k == 0:
            src, dst, to = buf.at[:, 1, INNER, :], row_r.at[base // 4, 1], (my_lat - 1, my_lon)
        elif k == 1:
            src, dst, to = buf.at[:, CLAT, INNER, :], row_r.at[base // 4, 0], (my_lat + 1, my_lon)
        elif k == 2:
            src, dst, to = edge_s.at[base // 4, 0], edge_r.at[base // 4, 1], (my_lat, my_lon - 1)
        else:
            src, dst, to = edge_s.at[base // 4, 1], edge_r.at[base // 4, 0], (my_lat, my_lon + 1)
        return pltpu.make_async_remote_copy(
            src, dst, edge_ssem.at[n], edge_rsem.at[n], device_id=to, device_id_type=MESH
        )

    has = [my_lat > 0, my_lat < N_LAT - 1, my_lon > 0, my_lon < N_LON - 1]
    opposite = [1, 0, 3, 2]

    def send_edges(buf, base):
        for r in range(R):
            edge_s[base // 4, 0, r] = buf[r, pl.ds(1, CLAT), LEFT, :]
            edge_s[base // 4, 1, r] = buf[r, pl.ds(1, CLAT), LEFT + CLON - 1, :]
        for k in range(4):
            @pl.when(has[k])
            def _(k=k):
                edge(buf, k, base).start()

    def take_edges(buf, base):
        for k in range(4):
            @pl.when(has[k])
            def _(k=k):
                edge(buf, opposite[k], base).wait_recv()
                edge(buf, k, base).wait_send()
        for k, row in ((0, 0), (1, LAT_PAD - 1)):
            @pl.when(has[k])
            def _(k=k, row=row):
                for r in range(R):
                    buf[r, row, INNER, :] = row_r[base // 4, k, r]
        for k, column in ((2, LEFT - 1), (3, LEFT + CLON)):
            @pl.when(has[k])
            def _(k=k, column=column):
                for r in range(R):
                    buf[r, pl.ds(1, CLAT), column, :] = edge_r[base // 4, k - 2, r]

    loads[0].wait()
    send_edges(mp, 0)

    def build_selt(g, carry):
        rows = pl.ds(pl.multiple_of(g * 16, 16), 16)
        number = (row16 + g * 16).astype(F32)
        for j in range(8):
            lanes = jnp.broadcast_to(rowcol[j], (16, 128))
            selt[rows, j * 128 : (j + 1) * 128] = one(lanes == number).astype(BF16)
        return carry

    rowcol = [rowval[j * 128 : (j + 1) * 128, :].T[0:1, :] for j in range(8)]
    lax.fori_loop(0, 64, build_selt, 0, unroll=2)
    zbuf[...] = jnp.zeros_like(zbuf)
    terms[TILES * 16 : 1024, :] = jnp.zeros((1024 - TILES * 16, 256), BF16)

    settle(ids_all, recv_sem.at[0])
    asked = ids_all[...]
    mine = (asked >> 10) == me
    lat0 = jnp.min(jnp.where(mine, (asked >> 5) & 31, CLAT - 4))
    lon0 = jnp.min(jnp.where(mine, asked & 31, CLON - 4))
    patch = jnp.concatenate(
        [mp[r, lat0 + i + 1, pl.ds(LEFT + lon0, 8), :] for r in range(R) for i in range(4)], axis=0
    ).astype(BF16)

    sub3 = iota((16, 8, 128), 1)
    lane3 = iota((16, 8, 128), 2)
    sign3 = jnp.where(sub3 < 4, 1.0, -1.0)

    def turn(c):
        return lax.rem(my_lat + c, N_LAT)

    def serve(c, carry):
        group = turn(c)
        near = jnp.broadcast_to(ids_all[pl.ds(group * 16, 16)], (16, 8, 128))
        cell = (((near >> 5) & 31) - lat0) * 8 + ((near & 31) - lon0)
        key = (lane3 * 64 + cell).astype(F32) * sign3
        least = jnp.min(jnp.where((near >> 10) == me, key, 1e6), axis=2, keepdims=True)
        pick = jnp.abs(least).astype(jnp.int32)
        target = jnp.where(pick < 64 * 128, (sub3 & 3) * 32 + (pick & 63), -1)
        hot = one(lane3 == target).reshape(128, 128).astype(BF16)
        rows = pl.ds(pl.multiple_of(group * 128, 128), 128)
        oh[rows, :] = hot
        resp[pl.ds(group * 16, 16)] = dot(hot, patch).reshape(16, 8, 128).astype(BF16)

        def send(s, carry):
            other = group * 16 + lax.rem(my_lon + s, N_LON)

            @pl.when(other != me)
            def _():
                pltpu.make_async_remote_copy(
                    resp.at[other], fetched.at[me], send_sem.at[1], recv_sem.at[1],
                    device_id=place(other), device_id_type=MESH,
                ).start()

            return carry

        lax.fori_loop(0, N_LON, send, 0)
        return carry

    lax.fori_loop(0, N_LAT, serve, 0)
    fetched[me] = resp[me]

    take_edges(mp, 0)
    loads[1].wait()
    sums = []
    for r in range(R):
        alpha = rec_s[0, r]

        def stencil(row, acc, r=r, alpha=alpha):
            damp = DAMP_WEIGHT * laplace_slab(mp, r, row) - alpha * dv[r, row]
            dp[r, row + 1, INNER] = damp
            return acc + fold(damp * damp)

        sums.append(lax.fori_loop(0, CLAT, stencil, jnp.zeros((8, 128), F32), unroll=2))
    send_edges(dp, 4)
    for j in range(8):
        blk = oh[j * 128 : (j + 1) * 128, :].astype(F32)
        oht[:, j * 128 : (j + 1) * 128] = blk.T.astype(BF16)
    ray_old = jnp.concatenate(
        [ray_v[:, b * RAYS_BLK : (b + 1) * RAYS_BLK] for b in range(RBMAX)]
        + [jnp.zeros((R, RAYS_BLK), F32)],
        axis=0,
    )
    wide16 = iota((16, RAYS_BLK), 0)
    r16 = wide16 & 3
    alpha16 = jnp.where(
        r16 == 0, rec_s[0, 0], jnp.where(r16 == 1, rec_s[0, 1], jnp.where(r16 == 2, rec_s[0, 2], rec_s[0, 3]))
    )
    ray_scaled = alpha16 * ray_old
    live = ((wide16 // 4) * RAYS_BLK + iota((16, RAYS_BLK), 1)) < cnt_s[0, 0]
    loads[2].wait()

    settle(fetched, recv_sem.at[1])
    blocks = fetched[...].reshape(1024, 128)
    for j in range(4):
        rows = slice(j * 256, (j + 1) * 256)
        wts[rows, :] = dot(sel[rows, :], blocks).astype(BF16)

    def forward(t, acc):
        rows = pl.ds(pl.multiple_of(t * 16, 16), 16)
        return acc + lax.dot_general(
            wts[rows, :], sens[t], (((1,), (1,)), ((), ())), preferred_element_type=F32
        )

    traced = lax.fori_loop(0, TILES, forward, jnp.zeros((16, RAYS_BLK), F32), unroll=6)
    ray_bar = jnp.where(live, traced - ray_scaled, 0.0)
    ray_keep[...] = ray_bar
    ray_sq = ray_bar * ray_bar
    ray_sq = ray_sq[:, 0:128] + ray_sq[:, 128:256]
    message = jnp.zeros((1, 128), F32)
    for r in range(R):
        part = jnp.where((row16 & 3) == r, ray_sq, 0.0)
        part = part[0:8] + part[8:16] + sums[r]
        message = jnp.where(iota((1, 128), 1) == r, jnp.sum(part, keepdims=True), message)
    sum_a[...] = message
    share(sum_a, sums_a, 2)

    ray_low = ray_bar.astype(BF16)

    def adjoint(t, carry):
        term = dot(ray_low, sens[t])
        high = term.astype(BF16)
        rows = pl.ds(pl.multiple_of(t * 16, 16), 16)
        terms[rows, 0:128] = high
        terms[rows, 128:256] = (term - high.astype(F32)).astype(BF16)
        return carry

    lax.fori_loop(0, TILES, adjoint, 0, unroll=6)

    def give(c, carry):
        group = turn(c)
        rows = pl.ds(pl.multiple_of(group * 128, 128), 128)
        both = dot(selt[rows, :], terms[...])
        outg[pl.ds(group * 16, 16)] = (both[:, 0:128] + both[:, 128:256]).reshape(16, 8, 128)

        def send(s, carry):
            other = group * 16 + lax.rem(my_lon + s, N_LON)

            @pl.when(other != me)
            def _():
                pltpu.make_async_remote_copy(
                    outg.at[other], inc.at[me], send_sem.at[3], recv_sem.at[3],
                    device_id=place(other), device_id_type=MESH,
                ).start()

            return carry

        lax.fori_loop(0, N_LON, send, 0)
        return carry

    lax.fori_loop(0, N_LAT, give, 0)
    inc[me] = outg[me]

    take_edges(dp, 4)
    for r in range(R):

        def stencil2(row, carry, r=r):
            dv[r, row] = DAMP_WEIGHT * laplace_slab(dp, r, row)
            return carry

        lax.fori_loop(0, CLAT, stencil2, 0, unroll=2)

    settle(sums_a, recv_sem.at[2])
    lane_sum = jnp.sum(sums_a[...], axis=0)[:, 0:R]
    beta = jnp.sqrt(lane_sum / ROWS_ALL + EPSILON)
    inv_beta = 1.0 / beta
    rho_bar = rec_v[1:2, :]
    phi_bar = rec_v[2:3, :]
    rho = jnp.sqrt(rho_bar * rho_bar + beta * beta)
    cosine = rho_bar / rho
    sine = beta / rho

    settle(inc, recv_sem.at[3])
    arrived = inc[...].reshape(1024, 128)
    high = arrived.astype(BF16)
    low = (arrived - high.astype(F32)).astype(BF16)
    image = dot(oht[...], high) + dot(oht[...], low)
    for r in range(R):
        for i in range(4):
            zbuf[r, i, pl.ds(32, 8), :] = image[r * 32 + i * 8 : r * 32 + i * 8 + 8]

    message = jnp.zeros((1, 128), F32)
    for r in range(R):
        beta_r = beta[:, r : r + 1]
        inv_r = inv_beta[:, r : r + 1]

        def renew(row, acc, r=r, beta_r=beta_r, inv_r=inv_r):
            off = row - lat0
            pick = jnp.where((off >= 0) & (off < 4), off, 4)
            extra = zbuf[r, pick, pl.ds(32 - lon0, CLON), :]
            upd = (dv[r, row] + extra) * inv_r - beta_r * mp[r, row + 1, INNER]
            upd_o[r, row] = upd
            return acc + fold(upd * upd)

        acc = lax.fori_loop(0, CLAT, renew, jnp.zeros((8, 128), F32), unroll=2)
        message = jnp.where(iota((1, 128), 1) == r, jnp.sum(acc, keepdims=True), message)
    sum_b[...] = message
    share(sum_b, sums_b, 4)

    loads[3].wait()
    loads[4].wait()
    gain = cosine * phi_bar / rho
    for r in range(R):
        inv_r = inv_beta[:, r : r + 1]
        gain_r = gain[:, r : r + 1]

        def scale(row, carry, r=r, inv_r=inv_r, gain_r=gain_r):
            damp_o[r, row] = dp[r, row + 1, INNER] * inv_r
            sol_o[r, row] = sol_o[r, row] + gain_r * search_o[r, row]
            return carry

        lax.fori_loop(0, CLAT, scale, 0, unroll=2)
        for b in range(RBMAX):
            ray_o[r : r + 1, b * RAYS_BLK : (b + 1) * RAYS_BLK] = (
                ray_keep[4 * b + r : 4 * b + r + 1, :] * inv_r
            )

    settle(sums_b, recv_sem.at[4])
    alpha_new = jnp.sqrt(jnp.sum(sums_b[...], axis=0)[:, 0:R] / CELLS + EPSILON)
    inv_alpha = 1.0 / alpha_new
    back = sine * alpha_new / rho
    for r in range(R):
        coef_o[r : r + 1, :] = jnp.broadcast_to(inv_alpha[:, r : r + 1], (1, 128))
        coef_o[4 + r : 5 + r, :] = jnp.broadcast_to(back[:, r : r + 1], (1, 128))
    rec_o[0:1, :] = alpha_new
    rec_o[1:2, :] = -cosine * alpha_new
    rec_o[2:3, :] = sine * phi_bar
    settle(ids_all, send_sem.at[0])
    settle(fetched, send_sem.at[1])
    settle(sums_a, send_sem.at[2])
    settle(inc, send_sem.at[3])
    settle(sums_b, send_sem.at[4])


def finish_kernel(
    upd, damp, sol, search, coef, ray, rec,
    ray_out, damp_out, model_out, sol_out, search_out, rec_out,
    model_s, search_s, sem,
):
    copies = [
        pltpu.make_async_copy(damp, damp_out, sem.at[0]),
        pltpu.make_async_copy(sol, sol_out, sem.at[1]),
        pltpu.make_async_copy(ray, ray_out, sem.at[2]),
        pltpu.make_async_copy(rec, rec_out, sem.at[3]),
    ]
    for copy in copies:
        copy.start()
    for r in range(R):
        inv_r = coef[r : r + 1, :]
        back_r = coef[4 + r : 5 + r, :]

        def write(row, carry, r=r, inv_r=inv_r, back_r=back_r):
            model = upd[r, row] * inv_r
            model_s[r, row] = model
            search_s[r, row] = model - back_r * search[r, row]
            return carry

        lax.fori_loop(0, CLAT, write, 0, unroll=4)
        for src, dst, k in ((model_s, model_out, 4), (search_s, search_out, 8)):
            copy = pltpu.make_async_copy(src.at[r], dst.at[r], sem.at[k + r])
            copy.start()
            copies.append(copy)
    for copy in copies:
        copy.wait()


def per_device(
    sensitivity, block_ids, block_offsets, ray_counts, ray_vector, damping_vector, model_vector,
    solution, search, recurrence,
):
    field = (R, CLAT, CLON, DEPTH)
    vmem = pl.BlockSpec(memory_space=pltpu.VMEM)
    smem = pl.BlockSpec(memory_space=pltpu.SMEM)
    hbm = pl.BlockSpec(memory_space=pl.ANY)
    ids = block_ids.reshape(1, TILES)
    padded = (R, LAT_PAD, LON_PAD, DEPTH)
    middle = [
        pltpu.VMEM(field, F32), pltpu.VMEM(field, F32), pltpu.VMEM(field, F32), pltpu.VMEM(field, F32),
        pltpu.VMEM((8, 128), F32), pltpu.VMEM((R, RBMAX * RAYS_BLK), F32), pltpu.VMEM((3, R), F32),
    ]
    kept = pl.pallas_call(
        step_kernel,
        out_shape=middle,
        in_specs=[smem, smem, smem, smem, vmem, vmem, vmem, hbm, hbm, hbm, hbm, hbm],
        out_specs=[vmem] * 7,
        scratch_shapes=[
            pltpu.VMEM(padded, F32),
            pltpu.VMEM(padded, F32),
            pltpu.VMEM(field, F32),
            pltpu.VMEM((TILES, RAYS_BLK, DEPTH), BF16),
            pltpu.VMEM((1, 128), jnp.int32),
            pltpu.VMEM((NDEV, 1, 128), jnp.int32),
            pltpu.VMEM((64, 128), jnp.int32),
            pltpu.VMEM((64, 128), jnp.int32),
            pltpu.VMEM((1024, 128), F32),
            pltpu.VMEM((1024, 1024), BF16),
            pltpu.VMEM((1024, 1024), BF16),
            pltpu.VMEM((1024, 128), BF16),
            pltpu.VMEM((128, 1024), BF16),
            pltpu.VMEM((NDEV, 8, 128), BF16),
            pltpu.VMEM((NDEV, 8, 128), BF16),
            pltpu.VMEM((1024, 128), BF16),
            pltpu.VMEM((1024, 256), BF16),
            pltpu.VMEM((NDEV, 8, 128), F32),
            pltpu.VMEM((NDEV, 8, 128), F32),
            pltpu.VMEM((R, 5, 72, DEPTH), F32),
            pltpu.VMEM((1, 128), F32),
            pltpu.VMEM((NDEV, 1, 128), F32),
            pltpu.VMEM((1, 128), F32),
            pltpu.VMEM((NDEV, 1, 128), F32),
            pltpu.VMEM((2, 2, R, CLAT, DEPTH), F32),
            pltpu.VMEM((2, 2, R, CLAT, DEPTH), F32),
            pltpu.VMEM((2, 2, R, CLON, DEPTH), F32),
            pltpu.VMEM((16, RAYS_BLK), F32),
            pltpu.SemaphoreType.DMA((5,)),
            pltpu.SemaphoreType.DMA((5,)),
            pltpu.SemaphoreType.DMA((5,)),
            pltpu.SemaphoreType.DMA((8,)),
            pltpu.SemaphoreType.DMA((8,)),
        ],
        compiler_params=pltpu.CompilerParams(
            collective_id=0, has_side_effects=True, vmem_limit_bytes=48 * 1024 * 1024
        ),
        name="step",
    )(
        ids, block_offsets.reshape(1, RBMAX + 1), ray_counts, recurrence, ids, recurrence,
        ray_vector.reshape(R, RBMAX * RAYS_BLK), sensitivity.reshape(TILES, RAYS_BLK, DEPTH),
        damping_vector, model_vector, solution, search,
    )
    shapes = [(R, RBMAX * RAYS_BLK), field, field, field, field, (3, R)]
    ray_out, damp_out, model_out, sol_out, search_out, rec_out = pl.pallas_call(
        finish_kernel,
        out_shape=[jax.ShapeDtypeStruct(s, F32) for s in shapes],
        in_specs=[vmem] * 7,
        out_specs=[hbm] * 6,
        scratch_shapes=[
            pltpu.VMEM(field, F32), pltpu.VMEM(field, F32), pltpu.SemaphoreType.DMA((12,)),
        ],
        compiler_params=pltpu.CompilerParams(vmem_limit_bytes=24 * 1024 * 1024),
        name="finish",
    )(*kept)
    ray_out = ray_out.reshape(R, 1, 1, RBMAX * RAYS_BLK)
    return (ray_out, damp_out, model_out, sol_out, search_out, rec_out)


def solution(mesh):
    wide = P(None, "lat", "lon", None)
    return jax.shard_map(
        per_device,
        mesh=mesh,
        in_specs=(
            P("lat", "lon", None, None, None),
            P("lat", "lon", None),
            P("lat", "lon", None),
            P("lat", "lon"),
            wide,
            wide,
            wide,
            wide,
            wide,
            P(),
        ),
        out_specs=(wide, wide, wide, wide, wide, P()),
        check_vma=False,
    )
```

time: 289 us -> 70.5 us (0.24)
  blocking collectives: 133 us -> 0 us
  Pallas kernels: 0 us -> 67 us
  other arithmetic: 63.7 us -> 0 us
  starting transfers between devices: 51.4 us -> 0 us
  local copies, waits for them, and re-layouts: 33.1 us -> 1.92 us
  matrix products: 4.69 us -> 0 us
    psum x2 -> x0, blocking collectives: 133 us -> none  [the longest x1 68.6 us: per_device(): residual_sq = lax.psum(residual_sq, ('lat', 'lon'))]
    pallas_call x0 -> x2, Pallas kernels: none -> 67 us  [the longest x1 63.6 us: per_device(): pl.pallas_call(step_kernel, out_shape=middle, in_specs=[smem, smem, smem,...]
    scatter-add x1 -> x0, other arithmetic: 31.4 us -> none  [per_device(): jnp.zeros((columns_dev + 1, systems, depth), jnp.float32).at[wanted]]
    all_to_all x3 -> x0, starting transfers between devices: 31.2 us -> none  [the longest x1 11.5 us: per_device(): lax.all_to_all(request, ('lat', 'lon'), split_axis=0, concat_axis=0, tile...]
    ppermute x8 -> x0, starting transfers between devices: 20.2 us -> none  [the longest x4 11.7 us: with_halo(): lax.ppermute(tail, axis, [(i, (i + 1) % count) for i in range(ends)])]
    reduce_sum x3 -> x0, other arithmetic: 15.8 us -> none  [the longest x1 9.79 us: per_device(): jnp.sum(damp_bar * damp_bar, axis=(1, 2, 3))]
    unnamed x43 -> x2, local copies, waits for them, and re-layouts: 11.9 us -> 1.92 us
    scatter x2 -> x0, local copies, waits for them, and re-layouts: 7.65 us -> none  [the longest x1 6.89 us: per_device(): jnp.zeros((devices * capacity, systems, depth), jnp.float32).at[slot_index]]
  transfers between devices with their start and end apart: 11 -> 0, of which waited for: 0 -> 0; matrix products, arithmetic and copies ran while one was open for 27% -> 0% of each run, Pallas kernels for 0% -> 0%
where the time goes in v2:
time: 70.5 us; the launch traced here: 70.3 us
  Pallas kernels  67 us (95%)
  local copies, waits for them, and re-layouts  1.92 us (3%)
  between operations  1.29 us (2%)
    pallas_call x1, Pallas kernels, per_device(): pl.pallas_call(step_kernel, out_shape=middle, in_specs=[smem, smem, smem,...  63.6 us
    pallas_call x1, Pallas kernels, per_device(): pl.pallas_call(finish_kernel, out_shape=[jax.ShapeDtypeStruct(s, F32) for...  3.39 us
    unnamed x2, local copies, waits for them, and re-layouts  1.92 us

profile of v2, /device:TPU:1, one launch (start us, length us, event | category | flops | bytes accessed | tf_op | source)
XLA Modules:
  0.0 70.3 jit_solution(4977285743773460713)
XLA Ops:
  1.3 1.3 %copy.19 = f32[4,1,1,768]{3,0,1,2:T(4,128)} copy(f32[4,1,1,768]{3,2,1,0:T(1,128)} %param.14) | data formatting | bytes 24576
  2.6 63.6 %step.1 = (f32[4,32,32,128]{3,2,1,0:T(8,128)S(1)}, f32[4,32,32,128]{3,2,1,0:T(8,128)S(1)}, f32[4,32,32,128]{3,2,1,0:T(8,128)S(1)}, f32[4,32,32,128]{3,2,1,0:T(8,...) custom-call(s32[1,60]{1,0:T(1,128)} %bitcast.10, s32[1,4]{1,0:T(1,128)} %bitcast.12, ...), custom_call_target="tpu_custom_call" | custom-call | tf_op jit(solution)/shard_map/step/pallas_call | solution.py:486
  66.2 3.4 %finish.1 = (f32[4,768]{1,0:T(4,128)S(1)}, f32[4,32,32,128]{3,2,1,0:T(8,128)}, f32[4,32,32,128]{3,2,1,0:T(8,128)}, f32[4,32,32,128]{3,2,1,0:T(8,128)}, f32[4,32,32,128]{3,2,1,0:T(8,128)}, /*index=5*/f32[3,4]{1,0:T(4,128)}) custom-call(f32[4,32,32,128]{3,2,1,0:T(8,128)S(1)} %get-tuple-element.19.upd, f32[4,32,32,128]{3,2,1,0:T(8,128)S(1)} %get-tuple-element.20.damp, ...), custom_call_target="tpu_custom_call" | custom-call | tf_op jit(solution)/shard_map/finish/pallas_call | solution.py:536
  69.6 0.6 copy.16

commit v3 on v2

--- a/solution.py
+++ b/solution.py
@@ -60,7 +60,7 @@
     ids_s, off_s, cnt_s, rec_s, ids_v, rec_v, ray_v, sens_h, damp_h, model_h, sol_h, search_h,
     upd_o, damp_o, sol_o, search_o, coef_o, ray_o, rec_o,
     mp, dp, dv, sens, idrow, ids_all, idcol, slotcol, rowval, sel, selt, oh, oht,
-    resp, fetched, wts, terms, outg, inc, zbuf, sum_a, sums_a, sum_b, sums_b,
+    resp, fetched, wts, terms, outg, inc, zbuf, sum_a, part_a, row_a, sums_a, sum_b, part_b, row_b, sums_b,
     edge_s, edge_r, row_r, ray_keep,
     load_sem, send_sem, recv_sem, edge_ssem, edge_rsem,
 ):
@@ -68,17 +68,24 @@
     my_lon = lax.axis_index("lon")
     me = my_lat * N_LON + my_lon
 
-    def place(other):
-        return (other // N_LON, lax.rem(other, N_LON))
-
     barrier = pltpu.get_barrier_semaphore()
 
-    def greet(step, carry):
-        other = lax.rem(me + step, NDEV)
-        pl.semaphore_signal(barrier, inc=1, device_id=place(other), device_id_type=MESH)
-        return carry
-
-    lax.fori_loop(1, NDEV, greet, 0)
+    def along_lon(step):
+        return (my_lat, lax.rem(my_lon + step, N_LON))
+
+    def along_lat(step):
+        return (lax.rem(my_lat + step, N_LAT), my_lon)
+
+    def greet_lon(step, carry):
+        pl.semaphore_signal(barrier, inc=1, device_id=along_lon(step), device_id_type=MESH)
+        return carry
+
+    def greet_lat(step, carry):
+        pl.semaphore_signal(barrier, inc=1, device_id=along_lat(step), device_id_type=MESH)
+        return carry
+
+    lax.fori_loop(1, N_LON, greet_lon, 0, unroll=True)
+    lax.fori_loop(1, N_LAT, greet_lat, 0, unroll=True)
 
     loads = [
         pltpu.make_async_copy(model_h, mp.at[:, pl.ds(1, CLAT), INNER, :], load_sem.at[0]),
@@ -139,25 +146,24 @@
 
     lax.fori_loop(0, 64, build_sel, 0, unroll=2)
 
-    pl.semaphore_wait(barrier, NDEV - 1)
-
-    def share(src, dst, k):
+    pl.semaphore_wait(barrier, N_LON - 1 + N_LAT - 1)
+
+    def spread(src, dst, k, count, along):
         def send(step, carry):
-            other = lax.rem(me + step, NDEV)
             pltpu.make_async_remote_copy(
-                src, dst.at[me], send_sem.at[k], recv_sem.at[k],
-                device_id=place(other), device_id_type=MESH,
+                src, dst, send_sem.at[k], recv_sem.at[k],
+                device_id=along(step), device_id_type=MESH,
             ).start()
             return carry
 
-        lax.fori_loop(1, NDEV, send, 0)
-        dst[me] = src[...]
-
-    def settle(dst, sem):
-        most = dst.at[pl.ds(0, NDEV - 1)]
+        lax.fori_loop(1, count, send, 0, unroll=True)
+
+    def settle(dst, sem, rows=NDEV - 1):
+        most = dst.at[pl.ds(0, rows)]
         pltpu.make_async_copy(most, most, sem).wait()
 
-    share(idrow, ids_all, 0)
+    spread(idrow, ids_all.at[me], 0, N_LON, along_lon)
+    ids_all[me] = idrow[...]
 
     def edge(buf, k, base):
         n = base + k
@@ -202,6 +208,9 @@
                 for r in range(R):
                     buf[r, pl.ds(1, CLAT), column, :] = edge_r[base // 4, k - 2, r]
 
+    row_ids = ids_all.at[pl.ds(my_lat * N_LON, N_LON)]
+    settle(ids_all, recv_sem.at[0], N_LON - 1)
+    spread(row_ids, row_ids, 5, N_LAT, along_lat)
     loads[0].wait()
     send_edges(mp, 0)
 
@@ -218,7 +227,17 @@
     zbuf[...] = jnp.zeros_like(zbuf)
     terms[TILES * 16 : 1024, :] = jnp.zeros((1024 - TILES * 16, 256), BF16)
 
-    settle(ids_all, recv_sem.at[0])
+    def gather_lon(src, parts, k):
+        spread(src, parts.at[my_lon], k, N_LON, along_lon)
+        parts[my_lon] = src[...]
+
+    def gather_lat(row_sum, parts, totals, k):
+        settle(parts, recv_sem.at[k], N_LON - 1)
+        row_sum[...] = jnp.sum(parts[...], axis=0)
+        spread(row_sum, totals.at[my_lat], k + 4, N_LAT, along_lat)
+        totals[my_lat] = row_sum[...]
+
+    settle(ids_all, recv_sem.at[5], NDEV - N_LON)
     asked = ids_all[...]
     mine = (asked >> 10) == me
     lat0 = jnp.min(jnp.where(mine, (asked >> 5) & 31, CLAT - 4))
@@ -234,7 +253,18 @@
     def turn(c):
         return lax.rem(my_lat + c, N_LAT)
 
-    def serve(c, carry):
+    def deal(src, dst, k, group, first):
+        def send(s, carry):
+            lon = lax.rem(my_lon + s, N_LON)
+            pltpu.make_async_remote_copy(
+                src.at[group * N_LON + lon], dst.at[me], send_sem.at[k], recv_sem.at[k],
+                device_id=(group, lon), device_id_type=MESH,
+            ).start()
+            return carry
+
+        lax.fori_loop(first, N_LON, send, 0, unroll=True)
+
+    def serve(c, carry, first=0):
         group = turn(c)
         near = jnp.broadcast_to(ids_all[pl.ds(group * 16, 16)], (16, 8, 128))
         cell = (((near >> 5) & 31) - lat0) * 8 + ((near & 31) - lon0)
@@ -247,22 +277,11 @@
         oh[rows, :] = hot
         resp[pl.ds(group * 16, 16)] = dot(hot, patch).reshape(16, 8, 128).astype(BF16)
 
-        def send(s, carry):
-            other = group * 16 + lax.rem(my_lon + s, N_LON)
-
-            @pl.when(other != me)
-            def _():
-                pltpu.make_async_remote_copy(
-                    resp.at[other], fetched.at[me], send_sem.at[1], recv_sem.at[1],
-                    device_id=place(other), device_id_type=MESH,
-                ).start()
-
-            return carry
-
-        lax.fori_loop(0, N_LON, send, 0)
-        return carry
-
-    lax.fori_loop(0, N_LAT, serve, 0)
+        deal(resp, fetched, 1, group, first)
+        return carry
+
+    serve(0, 0, first=1)
+    lax.fori_loop(1, N_LAT, serve, 0)
     fetched[me] = resp[me]
 
     take_edges(mp, 0)
@@ -318,7 +337,7 @@
         part = part[0:8] + part[8:16] + sums[r]
         message = jnp.where(iota((1, 128), 1) == r, jnp.sum(part, keepdims=True), message)
     sum_a[...] = message
-    share(sum_a, sums_a, 2)
+    gather_lon(sum_a, part_a, 2)
 
     ray_low = ray_bar.astype(BF16)
 
@@ -331,29 +350,19 @@
         return carry
 
     lax.fori_loop(0, TILES, adjoint, 0, unroll=6)
-
-    def give(c, carry):
+    gather_lat(row_a, part_a, sums_a, 2)
+
+    def give(c, carry, first=0):
         group = turn(c)
         rows = pl.ds(pl.multiple_of(group * 128, 128), 128)
         both = dot(selt[rows, :], terms[...])
         outg[pl.ds(group * 16, 16)] = (both[:, 0:128] + both[:, 128:256]).reshape(16, 8, 128)
 
-        def send(s, carry):
-            other = group * 16 + lax.rem(my_lon + s, N_LON)
-
-            @pl.when(other != me)
-            def _():
-                pltpu.make_async_remote_copy(
-                    outg.at[other], inc.at[me], send_sem.at[3], recv_sem.at[3],
-                    device_id=place(other), device_id_type=MESH,
-                ).start()
-
-            return carry
-
-        lax.fori_loop(0, N_LON, send, 0)
-        return carry
-
-    lax.fori_loop(0, N_LAT, give, 0)
+        deal(outg, inc, 3, group, first)
+        return carry
+
+    give(0, 0, first=1)
+    lax.fori_loop(1, N_LAT, give, 0)
     inc[me] = outg[me]
 
     take_edges(dp, 4)
@@ -365,7 +374,7 @@
 
         lax.fori_loop(0, CLAT, stencil2, 0, unroll=2)
 
-    settle(sums_a, recv_sem.at[2])
+    settle(sums_a, recv_sem.at[6], N_LAT - 1)
     lane_sum = jnp.sum(sums_a[...], axis=0)[:, 0:R]
     beta = jnp.sqrt(lane_sum / ROWS_ALL + EPSILON)
     inv_beta = 1.0 / beta
@@ -400,10 +409,15 @@
         acc = lax.fori_loop(0, CLAT, renew, jnp.zeros((8, 128), F32), unroll=2)
         message = jnp.where(iota((1, 128), 1) == r, jnp.sum(acc, keepdims=True), message)
     sum_b[...] = message
-    share(sum_b, sums_b, 4)
+    gather_lon(sum_b, part_b, 4)
 
     loads[3].wait()
     loads[4].wait()
+    for r in range(R):
+        for b in range(RBMAX):
+            ray_o[r : r + 1, b * RAYS_BLK : (b + 1) * RAYS_BLK] = (
+                ray_keep[4 * b + r : 4 * b + r + 1, :] * inv_beta[:, r : r + 1]
+            )
     gain = cosine * phi_bar / rho
     for r in range(R):
         inv_r = inv_beta[:, r : r + 1]
@@ -415,12 +429,10 @@
             return carry
 
         lax.fori_loop(0, CLAT, scale, 0, unroll=2)
-        for b in range(RBMAX):
-            ray_o[r : r + 1, b * RAYS_BLK : (b + 1) * RAYS_BLK] = (
-                ray_keep[4 * b + r : 4 * b + r + 1, :] * inv_r
-            )
-
-    settle(sums_b, recv_sem.at[4])
+        if r == 1:
+            gather_lat(row_b, part_b, sums_b, 4)
+
+    settle(sums_b, recv_sem.at[8], N_LAT - 1)
     alpha_new = jnp.sqrt(jnp.sum(sums_b[...], axis=0)[:, 0:R] / CELLS + EPSILON)
     inv_alpha = 1.0 / alpha_new
     back = sine * alpha_new / rho
@@ -430,11 +442,14 @@
     rec_o[0:1, :] = alpha_new
     rec_o[1:2, :] = -cosine * alpha_new
     rec_o[2:3, :] = sine * phi_bar
-    settle(ids_all, send_sem.at[0])
+    settle(ids_all, send_sem.at[0], N_LON - 1)
+    settle(ids_all, send_sem.at[5], NDEV - N_LON)
     settle(fetched, send_sem.at[1])
-    settle(sums_a, send_sem.at[2])
+    settle(part_a, send_sem.at[2], N_LON - 1)
+    settle(sums_a, send_sem.at[6], N_LAT - 1)
     settle(inc, send_sem.at[3])
-    settle(sums_b, send_sem.at[4])
+    settle(part_b, send_sem.at[4], N_LON - 1)
+    settle(sums_b, send_sem.at[8], N_LAT - 1)
 
 
 def finish_kernel(
@@ -510,16 +525,20 @@
             pltpu.VMEM((NDEV, 8, 128), F32),
             pltpu.VMEM((R, 5, 72, DEPTH), F32),
             pltpu.VMEM((1, 128), F32),
-            pltpu.VMEM((NDEV, 1, 128), F32),
+            pltpu.VMEM((N_LON, 1, 128), F32),
             pltpu.VMEM((1, 128), F32),
-            pltpu.VMEM((NDEV, 1, 128), F32),
+            pltpu.VMEM((N_LAT, 1, 128), F32),
+            pltpu.VMEM((1, 128), F32),
+            pltpu.VMEM((N_LON, 1, 128), F32),
+            pltpu.VMEM((1, 128), F32),
+            pltpu.VMEM((N_LAT, 1, 128), F32),
             pltpu.VMEM((2, 2, R, CLAT, DEPTH), F32),
             pltpu.VMEM((2, 2, R, CLAT, DEPTH), F32),
             pltpu.VMEM((2, 2, R, CLON, DEPTH), F32),
             pltpu.VMEM((16, RAYS_BLK), F32),
             pltpu.SemaphoreType.DMA((5,)),
-            pltpu.SemaphoreType.DMA((5,)),
-            pltpu.SemaphoreType.DMA((5,)),
+            pltpu.SemaphoreType.DMA((9,)),
+            pltpu.SemaphoreType.DMA((9,)),
             pltpu.SemaphoreType.DMA((8,)),
             pltpu.SemaphoreType.DMA((8,)),
         ],

time: 70.5 us -> 66.2 us (0.939)
  Pallas kernels: 67 us -> 62.8 us
    pallas_call x1, Pallas kernels: 63.6 us -> 59.4 us  [per_device(): pl.pallas_call(step_kernel, out_shape=middle, in_specs=[smem, smem, smem,...]
where the time goes in v3:
time: 66.2 us; the launch traced here: 66 us
  Pallas kernels  62.8 us (95%)
  local copies, waits for them, and re-layouts  1.92 us (3%)
  between operations  1.29 us (2%)
    pallas_call x1, Pallas kernels, per_device(): pl.pallas_call(step_kernel, out_shape=middle, in_specs=[smem, smem, smem,...  59.4 us
    pallas_call x1, Pallas kernels, per_device(): pl.pallas_call(finish_kernel, out_shape=[jax.ShapeDtypeStruct(s, F32) for...  3.39 us
    unnamed x2, local copies, waits for them, and re-layouts  1.92 us

profile of v3, /device:TPU:1, one launch (start us, length us, event | category | flops | bytes accessed | tf_op | source)
XLA Modules:
  0.0 66.0 jit_solution(2930124665163500891)
XLA Ops:
  1.3 1.3 %copy.19 = f32[4,1,1,768]{3,0,1,2:T(4,128)} copy(f32[4,1,1,768]{3,2,1,0:T(1,128)} %param.14) | data formatting | bytes 24576
  2.6 59.4 %step.1 = (f32[4,32,32,128]{3,2,1,0:T(8,128)S(1)}, f32[4,32,32,128]{3,2,1,0:T(8,128)S(1)}, f32[4,32,32,128]{3,2,1,0:T(8,128)S(1)}, f32[4,32,32,128]{3,2,1,0:T(8,...) custom-call(s32[1,60]{1,0:T(1,128)} %bitcast.10, s32[1,4]{1,0:T(1,128)} %bitcast.12, ...), custom_call_target="tpu_custom_call" | custom-call | tf_op jit(solution)/shard_map/step/pallas_call | solution.py:501
  62.0 3.4 %finish.1 = (f32[4,768]{1,0:T(4,128)S(1)}, f32[4,32,32,128]{3,2,1,0:T(8,128)}, f32[4,32,32,128]{3,2,1,0:T(8,128)}, f32[4,32,32,128]{3,2,1,0:T(8,128)}, f32[4,32,32,128]{3,2,1,0:T(8,128)}, /*index=5*/f32[3,4]{1,0:T(4,128)}) custom-call(f32[4,32,32,128]{3,2,1,0:T(8,128)S(1)} %get-tuple-element.19.upd, f32[4,32,32,128]{3,2,1,0:T(8,128)S(1)} %get-tuple-element.20.damp, ...), custom_call_target="tpu_custom_call" | custom-call | tf_op jit(solution)/shard_map/finish/pallas_call | solution.py:555
  65.4 0.6 copy.16

commit v4 on v3

--- a/solution.py
+++ b/solution.py
@@ -94,8 +94,8 @@
         pltpu.make_async_copy(sol_h, sol_o, load_sem.at[3]),
         pltpu.make_async_copy(search_h, search_o, load_sem.at[4]),
     ]
-    for load in loads:
-        load.start()
+    loads[0].start()
+    loads[1].start()
 
     idrow[...] = jnp.full((1, 128), -1, jnp.int32)
     idrow[:, 0:TILES] = ids_v[...]
@@ -208,12 +208,6 @@
                 for r in range(R):
                     buf[r, pl.ds(1, CLAT), column, :] = edge_r[base // 4, k - 2, r]
 
-    row_ids = ids_all.at[pl.ds(my_lat * N_LON, N_LON)]
-    settle(ids_all, recv_sem.at[0], N_LON - 1)
-    spread(row_ids, row_ids, 5, N_LAT, along_lat)
-    loads[0].wait()
-    send_edges(mp, 0)
-
     def build_selt(g, carry):
         rows = pl.ds(pl.multiple_of(g * 16, 16), 16)
         number = (row16 + g * 16).astype(F32)
@@ -224,6 +218,12 @@
 
     rowcol = [rowval[j * 128 : (j + 1) * 128, :].T[0:1, :] for j in range(8)]
     lax.fori_loop(0, 64, build_selt, 0, unroll=2)
+    row_ids = ids_all.at[pl.ds(my_lat * N_LON, N_LON)]
+    settle(ids_all, recv_sem.at[0], N_LON - 1)
+    spread(row_ids, row_ids, 5, N_LAT, along_lat)
+    loads[0].wait()
+    loads[2].start()
+    send_edges(mp, 0)
     zbuf[...] = jnp.zeros_like(zbuf)
     terms[TILES * 16 : 1024, :] = jnp.zeros((1024 - TILES * 16, 256), BF16)
 
@@ -255,7 +255,7 @@
 
     def deal(src, dst, k, group, first):
         def send(s, carry):
-            lon = lax.rem(my_lon + s, N_LON)
+            lon = lax.rem(my_lon + 5 * s, N_LON)
             pltpu.make_async_remote_copy(
                 src.at[group * N_LON + lon], dst.at[me], send_sem.at[k], recv_sem.at[k],
                 device_id=(group, lon), device_id_type=MESH,
@@ -283,6 +283,8 @@
     serve(0, 0, first=1)
     lax.fori_loop(1, N_LAT, serve, 0)
     fetched[me] = resp[me]
+    loads[3].start()
+    loads[4].start()
 
     take_edges(mp, 0)
     loads[1].wait()
@@ -301,7 +303,7 @@
         blk = oh[j * 128 : (j + 1) * 128, :].astype(F32)
         oht[:, j * 128 : (j + 1) * 128] = blk.T.astype(BF16)
     ray_old = jnp.concatenate(
-        [ray_v[:, b * RAYS_BLK : (b + 1) * RAYS_BLK] for b in range(RBMAX)]
+        [ray_v[r, 0, :, b * RAYS_BLK : (b + 1) * RAYS_BLK] for b in range(RBMAX) for r in range(R)]
         + [jnp.zeros((R, RAYS_BLK), F32)],
         axis=0,
     )
@@ -350,7 +352,6 @@
         return carry
 
     lax.fori_loop(0, TILES, adjoint, 0, unroll=6)
-    gather_lat(row_a, part_a, sums_a, 2)
 
     def give(c, carry, first=0):
         group = turn(c)
@@ -364,6 +365,7 @@
     give(0, 0, first=1)
     lax.fori_loop(1, N_LAT, give, 0)
     inc[me] = outg[me]
+    gather_lat(row_a, part_a, sums_a, 2)
 
     take_edges(dp, 4)
     for r in range(R):
@@ -415,7 +417,7 @@
     loads[4].wait()
     for r in range(R):
         for b in range(RBMAX):
-            ray_o[r : r + 1, b * RAYS_BLK : (b + 1) * RAYS_BLK] = (
+            ray_o[r, 0, :, b * RAYS_BLK : (b + 1) * RAYS_BLK] = (
                 ray_keep[4 * b + r : 4 * b + r + 1, :] * inv_beta[:, r : r + 1]
             )
     gain = cosine * phi_bar / rho
@@ -496,7 +498,7 @@
     padded = (R, LAT_PAD, LON_PAD, DEPTH)
     middle = [
         pltpu.VMEM(field, F32), pltpu.VMEM(field, F32), pltpu.VMEM(field, F32), pltpu.VMEM(field, F32),
-        pltpu.VMEM((8, 128), F32), pltpu.VMEM((R, RBMAX * RAYS_BLK), F32), pltpu.VMEM((3, R), F32),
+        pltpu.VMEM((8, 128), F32), pltpu.VMEM((R, 1, 1, RBMAX * RAYS_BLK), F32), pltpu.VMEM((3, R), F32),
     ]
     kept = pl.pallas_call(
         step_kernel,
@@ -548,10 +550,10 @@
         name="step",
     )(
         ids, block_offsets.reshape(1, RBMAX + 1), ray_counts, recurrence, ids, recurrence,
-        ray_vector.reshape(R, RBMAX * RAYS_BLK), sensitivity.reshape(TILES, RAYS_BLK, DEPTH),
+        ray_vector, sensitivity.reshape(TILES, RAYS_BLK, DEPTH),
         damping_vector, model_vector, solution, search,
     )
-    shapes = [(R, RBMAX * RAYS_BLK), field, field, field, field, (3, R)]
+    shapes = [(R, 1, 1, RBMAX * RAYS_BLK), field, field, field, field, (3, R)]
     ray_out, damp_out, model_out, sol_out, search_out, rec_out = pl.pallas_call(
         finish_kernel,
         out_shape=[jax.ShapeDtypeStruct(s, F32) for s in shapes],
@@ -563,7 +565,6 @@
         compiler_params=pltpu.CompilerParams(vmem_limit_bytes=24 * 1024 * 1024),
         name="finish",
     )(*kept)
-    ray_out = ray_out.reshape(R, 1, 1, RBMAX * RAYS_BLK)
     return (ray_out, damp_out, model_out, sol_out, search_out, rec_out)
 
 

time: 66.2 us -> 62.6 us (0.946)
  local copies, waits for them, and re-layouts: 1.92 us -> 0 us
  Pallas kernels: 62.8 us -> 61.2 us
    unnamed x2 -> x0, local copies, waits for them, and re-layouts: 1.92 us -> none
    pallas_call x1, Pallas kernels: 59.4 us -> 57.8 us  [per_device(): pl.pallas_call(step_kernel, out_shape=middle, in_specs=[smem, smem, smem,...]
where the time goes in v4:
time: 62.6 us; the launch traced here: 62.4 us
  Pallas kernels  61.2 us (98%)
  between operations  1.29 us (2%)
    pallas_call x1, Pallas kernels, per_device(): pl.pallas_call(step_kernel, out_shape=middle, in_specs=[smem, smem, smem,...  57.8 us
    pallas_call x1, Pallas kernels, per_device(): pl.pallas_call(finish_kernel, out_shape=[jax.ShapeDtypeStruct(s, F32) for...  3.39 us

profile of v4, /device:TPU:1, one launch (start us, length us, event | category | flops | bytes accessed | tf_op | source)
XLA Modules:
  0.0 62.4 jit_solution(15961199028210857917)
XLA Ops:
  1.3 57.8 %step.1 = (f32[4,32,32,128]{3,2,1,0:T(8,128)S(1)}, f32[4,32,32,128]{3,2,1,0:T(8,128)S(1)}, f32[4,32,32,128]{3,2,1,0:T(8,128)S(1)}, f32[4,32,32,128]{3,2,1,0:T(8,...) custom-call(s32[1,60]{1,0:T(1,128)} %bitcast.4, s32[1,4]{1,0:T(1,128)} %bitcast.6, ...), custom_call_target="tpu_custom_call" | custom-call | tf_op jit(solution)/shard_map/step/pallas_call | solution.py:503
  59.0 3.4 %finish.1 = (f32[4,1,1,768]{3,2,1,0:T(1,128)}, f32[4,32,32,128]{3,2,1,0:T(8,128)}, f32[4,32,32,128]{3,2,1,0:T(8,128)}, f32[4,32,32,128]{3,2,1,0:T(8,128)}, f32[4,32,32,128]{3,2,1,0:T(8,128)}, /*index=5*/f32[3,4]{1,0:T(4,128)}) custom-call(f32[4,32,32,128]{3,2,1,0:T(8,128)S(1)} %get-tuple-element.13.upd, f32[4,32,32,128]{3,2,1,0:T(8,128)S(1)} %get-tuple-element.14.damp, ...), custom_call_target="tpu_custom_call" | custom-call | tf_op jit(solution)/shard_map/finish/pallas_call | solution.py:557

commit v5 on v4

--- a/solution.py
+++ b/solution.py
@@ -251,7 +251,7 @@
     sign3 = jnp.where(sub3 < 4, 1.0, -1.0)
 
     def turn(c):
-        return lax.rem(my_lat + c, N_LAT)
+        return lax.rem(my_lat + 1 + lax.rem(c + 3, N_LAT - 1), N_LAT)
 
     def deal(src, dst, k, group, first):
         def send(s, carry):
@@ -265,7 +265,7 @@
         lax.fori_loop(first, N_LON, send, 0, unroll=True)
 
     def serve(c, carry, first=0):
-        group = turn(c)
+        group = my_lat if first else turn(c)
         near = jnp.broadcast_to(ids_all[pl.ds(group * 16, 16)], (16, 8, 128))
         cell = (((near >> 5) & 31) - lat0) * 8 + ((near & 31) - lon0)
         key = (lane3 * 64 + cell).astype(F32) * sign3
@@ -280,8 +280,8 @@
         deal(resp, fetched, 1, group, first)
         return carry
 
-    serve(0, 0, first=1)
-    lax.fori_loop(1, N_LAT, serve, 0)
+    lax.fori_loop(0, N_LAT - 1, serve, 0)
+    serve(None, 0, first=1)
     fetched[me] = resp[me]
     loads[3].start()
     loads[4].start()
@@ -354,7 +354,7 @@
     lax.fori_loop(0, TILES, adjoint, 0, unroll=6)
 
     def give(c, carry, first=0):
-        group = turn(c)
+        group = my_lat if first else turn(c)
         rows = pl.ds(pl.multiple_of(group * 128, 128), 128)
         both = dot(selt[rows, :], terms[...])
         outg[pl.ds(group * 16, 16)] = (both[:, 0:128] + both[:, 128:256]).reshape(16, 8, 128)
@@ -362,8 +362,8 @@
         deal(outg, inc, 3, group, first)
         return carry
 
-    give(0, 0, first=1)
-    lax.fori_loop(1, N_LAT, give, 0)
+    lax.fori_loop(0, N_LAT - 1, give, 0)
+    give(None, 0, first=1)
     inc[me] = outg[me]
     gather_lat(row_a, part_a, sums_a, 2)
 

time: 62.6 us -> 61.5 us (0.982)
  Pallas kernels: 61.2 us -> 60.1 us
    pallas_call x1, Pallas kernels: 57.8 us -> 56.7 us  [per_device(): pl.pallas_call(step_kernel, out_shape=middle, in_specs=[smem, smem, smem,...]
where the time goes in v5:
time: 61.5 us; the launch traced here: 61.3 us
  Pallas kernels  60.1 us (98%)
  between operations  1.29 us (2%)
    pallas_call x1, Pallas kernels, per_device(): pl.pallas_call(step_kernel, out_shape=middle, in_specs=[smem, smem, smem,...  56.7 us
    pallas_call x1, Pallas kernels, per_device(): pl.pallas_call(finish_kernel, out_shape=[jax.ShapeDtypeStruct(s, F32) for...  3.39 us

profile of v5, /device:TPU:1, one launch (start us, length us, event | category | flops | bytes accessed | tf_op | source)
XLA Modules:
  0.0 61.3 jit_solution(14855478594584872068)
XLA Ops:
  1.3 56.7 %step.1 = (f32[4,32,32,128]{3,2,1,0:T(8,128)S(1)}, f32[4,32,32,128]{3,2,1,0:T(8,128)S(1)}, f32[4,32,32,128]{3,2,1,0:T(8,128)S(1)}, f32[4,32,32,128]{3,2,1,0:T(8,...) custom-call(s32[1,60]{1,0:T(1,128)} %bitcast.4, s32[1,4]{1,0:T(1,128)} %bitcast.6, ...), custom_call_target="tpu_custom_call" | custom-call | tf_op jit(solution)/shard_map/step/pallas_call | solution.py:503
  58.0 3.4 %finish.1 = (f32[4,1,1,768]{3,2,1,0:T(1,128)}, f32[4,32,32,128]{3,2,1,0:T(8,128)}, f32[4,32,32,128]{3,2,1,0:T(8,128)}, f32[4,32,32,128]{3,2,1,0:T(8,128)}, f32[4,32,32,128]{3,2,1,0:T(8,128)}, /*index=5*/f32[3,4]{1,0:T(4,128)}) custom-call(f32[4,32,32,128]{3,2,1,0:T(8,128)S(1)} %get-tuple-element.13.upd, f32[4,32,32,128]{3,2,1,0:T(8,128)S(1)} %get-tuple-element.14.damp, ...), custom_call_target="tpu_custom_call" | custom-call | tf_op jit(solution)/shard_map/finish/pallas_call | solution.py:557
